TPU v7x, 512 devices: a whole 4x4x16 slice. The times are simulated.
512 devices in a mesh: au: 16 (over y, x), vert: 32 (over z, core).
Axes of the slice: x: 4, y: 4, z: 16, core: 2. Of those that a mesh axis runs over, the one named last changes fastest.
Arguments:
- visibilities: bfloat16 [12288, 2, 2048], P(('au', 'vert')), may hold values from -6 to 6
- baseline_offsets: float32 [12288, 2, 128], P(('au', 'vert')), may hold values from -8 to 8
- channel_scale: float32 [16], replicated, may hold values from 0.8 to 1.25
- screen_depth: float32 [12288], P(('au', 'vert')), may hold values from -300 to 300
- stations: int32 [12288, 2], P(('au', 'vert')), may hold values from 0 to 511
- corners: int32 [12288, 2], P(('au', 'vert')), may hold values from 0 to 8191, as said below
- beam_terms: bfloat16 [512, 2, 1024], P(('au', 'vert')), may hold values from -5 to 5
Outputs:
- gridded: float32 [8192, 2, 8192], P('au', None, 'vert')
- dirty_image: float32 [8192, 2, 8192], P(('au', 'vert'))
Inputs may be any that keep to these rules, and one draw needn't show every extreme that they name: Subgrid s belongs to block d = floor(s / 24); with d = r * 32 + c, corners[s, 0] lies in [r * 512, (r + 1) * 512) and the columns corners[s, 1] to corners[s, 1] + 31 lie inside one column tile of 256 columns. At most 2 subgrids of one block lie in one column tile; for every r one column tile holds exactly 2 subgrids of every block of that r.
All inputs are finite; a program needn't handle non-finite values.
Results may differ from a plain program's by a relative error of at most 0.039.
Values may be sent and summed in bfloat16 or wider, within the bound.
A program may use at most 64 MiB of HBM per device.

v0:
```python
import math

import jax
import jax.numpy as jnp
from jax import lax
from jax.sharding import PartitionSpec as P

G = 8192
SUB = 32


field_view = 0.1
highest = lax.Precision.HIGHEST


def passed_along(value, axis, steps):
    count = lax.axis_size(axis)
    pairs = [(source, (source + steps) % count) for source in range(count)]
    return lax.ppermute(value, axis, pairs)


def complex_einsum(formula, left_operand_pair, right_pair):
    left_re, left_im = left_operand_pair
    right_re, right_im = right_pair
    real_part = jnp.einsum(formula, left_re, right_re, precision=highest) - jnp.einsum(
        formula, left_im, right_im, precision=highest
    )
    imag_part = jnp.einsum(formula, left_re, right_im, precision=highest) + jnp.einsum(
        formula, left_im, right_re, precision=highest
    )
    return (real_part, imag_part)


def complex_product(left_operand_pair, right_pair):
    return (
        left_operand_pair[0] * right_pair[0] - left_operand_pair[1] * right_pair[1],
        left_operand_pair[0] * right_pair[1] + left_operand_pair[1] * right_pair[0],
    )


def unit_table(row_count, col_count, period):
    product = (
        jnp.arange(row_count, dtype=jnp.int32)[:, None]
        * jnp.arange(col_count, dtype=jnp.int32)[None, :]
        % period
    )
    angle = 2.0 * math.pi / period * product.astype(jnp.float32)
    return (jnp.cos(angle), jnp.sin(angle))


def subgrid_table():
    centred = jnp.arange(SUB, dtype=jnp.int32) - SUB // 2
    product = centred[:, None] * centred[None, :] % SUB
    angle = -2.0 * math.pi / SUB * product.astype(jnp.float32)
    return (jnp.cos(angle) / SUB, jnp.sin(angle) / SUB)


def grid_subgrids(vis_items, offset_items, depth_items, beam_first, beam_second, channel_scale):
    item_count = vis_items.shape[0]
    vis_count = vis_items.shape[2]
    pixel_pos = jnp.arange(SUB, dtype=jnp.float32) - SUB // 2
    shift_u = (offset_items[:, 0, :, None] * channel_scale[None, None, :]).reshape(
        item_count, vis_count
    )
    shift_v = (offset_items[:, 1, :, None] * channel_scale[None, None, :]).reshape(
        item_count, vis_count
    )
    angle_u = 2.0 * math.pi / SUB * pixel_pos[None, :, None] * shift_u[:, None, :]
    angle_v = 2.0 * math.pi / SUB * pixel_pos[None, :, None] * shift_v[:, None, :]
    vis_re = vis_items[:, 0, None, :].astype(jnp.float32)
    vis_im = vis_items[:, 1, None, :].astype(jnp.float32)
    cos_u = jnp.cos(angle_u)
    sin_u = jnp.sin(angle_u)
    weighted_re = (vis_re * cos_u - vis_im * sin_u).astype(jnp.bfloat16)
    weighted_im = (vis_re * sin_u + vis_im * cos_u).astype(jnp.bfloat16)
    phasor_re = jnp.cos(angle_v).astype(jnp.bfloat16)
    phasor_im = jnp.sin(angle_v).astype(jnp.bfloat16)
    stacked_left = jnp.concatenate([weighted_re, weighted_im], axis=2)
    stacked_right = jnp.concatenate(
        [
            jnp.concatenate([phasor_re, -phasor_im], axis=2),
            jnp.concatenate([phasor_im, phasor_re], axis=2),
        ],
        axis=1,
    )
    sky_both = jnp.einsum(
        "npk,nqk->npq", stacked_left, stacked_right, preferred_element_type=jnp.float32
    )
    sky_pair = (sky_both[:, :, :SUB], sky_both[:, :, SUB:])
    taper_line = 1.0 - ((2.0 * jnp.arange(SUB, dtype=jnp.float32) + 1.0 - SUB) / SUB) ** 2
    taper_grid = taper_line[:, None] * taper_line[None, :] / math.sqrt(vis_count)
    sky_angle = pixel_pos * field_view / SUB
    radius_sq = sky_angle[:, None] ** 2 + sky_angle[None, :] ** 2
    screen_angle = -math.pi * depth_items[:, None, None] * radius_sq[None, :, :]
    first_beam = beam_first.astype(jnp.float32).reshape(item_count, 2, SUB, SUB)
    second_beam = beam_second.astype(jnp.float32).reshape(item_count, 2, SUB, SUB)
    pair_term = complex_product(
        (first_beam[:, 0], first_beam[:, 1]), (second_beam[:, 0], -second_beam[:, 1])
    )
    mixed = complex_product(sky_pair, pair_term)
    screened = complex_product(mixed, (jnp.cos(screen_angle), jnp.sin(screen_angle)))
    corrected = (screened[0] * taper_grid, screened[1] * taper_grid)
    dft_pair = subgrid_table()
    partial_pair = complex_einsum("ip,npq->niq", dft_pair, corrected)
    uv_pair = complex_einsum("niq,jq->nij", partial_pair, dft_pair)
    return jnp.stack(uv_pair, axis=1).reshape(item_count, 2 * SUB * SUB)


def grid_in_blocks(vis_items, offset_items, depth_items, first_items, second_items, channel_scale):
    item_count = vis_items.shape[0]
    block_size = math.gcd(item_count, 4)
    block_count = item_count // block_size

    def regroup(source):
        return source.reshape((block_count, block_size) + source.shape[1:])

    def grid_block(pieces):
        return grid_subgrids(
            pieces[0], pieces[1], pieces[2], pieces[3], pieces[4], channel_scale
        ).astype(jnp.bfloat16)

    gridded_blocks = lax.map(
        grid_block,
        (
            regroup(vis_items),
            regroup(offset_items),
            regroup(depth_items),
            regroup(first_items),
            regroup(second_items),
        ),
    )
    return gridded_blocks.reshape(item_count, 2 * SUB * SUB)


def add_subgrids(uv_items, offset_items, tile_rows, tile_cols):
    item_count = uv_items.shape[0]
    pieces = uv_items.reshape(item_count, 2, SUB, SUB)
    span_index = jnp.arange(SUB, dtype=jnp.int32)
    column_index = jnp.arange(tile_cols, dtype=jnp.int32)
    column_onehot = (
        column_index[None, None, :] == offset_items[:, 1, None, None] + span_index[None, :, None]
    ).astype(jnp.bfloat16)
    placed = jnp.einsum("mcij,mjv->micv", pieces, column_onehot, preferred_element_type=jnp.float32)
    row_ids = (offset_items[:, 0, None] + span_index[None, :]).reshape(-1)
    return jax.ops.segment_sum(
        placed.reshape(item_count * SUB, 2 * tile_cols), row_ids, num_segments=tile_rows + SUB
    )


def on_device(
    visibilities, baseline_offsets, channel_scale, screen_depth, stations, corners, beam_terms
):
    au_count = lax.axis_size("au")
    vertical_count = lax.axis_size("vert")
    device_count = au_count * vertical_count
    tile_rows = G // au_count
    tile_cols = G // vertical_count
    own_count = visibilities.shape[0]
    capacity = max(2, (2 * own_count + vertical_count - 1) // vertical_count)
    slot_count = vertical_count * capacity
    beam_table = lax.all_gather(beam_terms, ("au", "vert"), axis=0, tiled=True)
    target = corners[:, 1] // tile_cols
    row_offset = corners[:, 0] - lax.axis_index("au") * tile_rows
    col_offset = corners[:, 1] - target * tile_cols
    offsets = jnp.stack([row_offset, col_offset], axis=1)
    chosen = (target[:, None] == jnp.arange(vertical_count, dtype=jnp.int32)[None, :]).astype(
        jnp.int32
    )
    order_index = jnp.arange(own_count, dtype=jnp.int32)
    earlier_mask = (order_index[None, :] < order_index[:, None]).astype(jnp.int32)
    earlier_count = jnp.dot(earlier_mask, chosen)
    slot_rank = jnp.sum(chosen * earlier_count, axis=1)
    slot_index = target * capacity + slot_rank
    placement = jnp.arange(slot_count, dtype=jnp.int32)[:, None] == slot_index[None, :]
    place_whole = placement.astype(jnp.int32)
    uv_items = grid_in_blocks(
        visibilities,
        baseline_offsets,
        screen_depth,
        jnp.take(beam_table, stations[:, 0], axis=0),
        jnp.take(beam_table, stations[:, 1], axis=0),
        channel_scale,
    )
    uv_send = (
        jnp.dot(placement.astype(jnp.bfloat16), uv_items, preferred_element_type=jnp.float32)
        .astype(jnp.bfloat16)
        .reshape(vertical_count, capacity, -1)
    )
    offset_send = jnp.dot(place_whole, offsets).reshape(vertical_count, capacity, 2)
    uv_slots, offset_slots = (
        lax.all_to_all(uv_send, "vert", split_axis=0, concat_axis=0, tiled=True),
        lax.all_to_all(offset_send, "vert", split_axis=0, concat_axis=0, tiled=True),
    )
    extended = add_subgrids(
        uv_slots.reshape(slot_count, 2 * SUB * SUB),
        offset_slots.reshape(slot_count, 2),
        tile_rows,
        tile_cols,
    )
    carried = passed_along(extended[tile_rows:].astype(jnp.bfloat16), "au", 1).astype(jnp.float32)
    uv_tile = extended[:tile_rows].at[:SUB].add(carried).reshape(tile_rows, 2, tile_cols)
    block_rows = G // device_count
    row_blocks = lax.all_to_all(
        uv_tile.astype(jnp.bfloat16), "vert", split_axis=0, concat_axis=2, tiled=True
    ).astype(uv_tile.dtype)
    split_rows = row_blocks.reshape(block_rows, 2, block_rows, device_count)
    short_table = unit_table(block_rows, block_rows, block_rows)
    long_table = unit_table(device_count, device_count, device_count)
    twist_cols = unit_table(block_rows, device_count, G)
    first_pass = complex_einsum("urj,kr->ukj", (split_rows[:, 0], split_rows[:, 1]), short_table)
    first_pass = complex_product(first_pass, (twist_cols[0][None], twist_cols[1][None]))
    second_pass = complex_einsum("ukj,pj->pku", first_pass, long_table)
    spectra = jnp.stack(second_pass, axis=1).reshape(
        au_count, vertical_count, 2, block_rows * block_rows
    )
    arrived = lax.all_to_all(
        lax.all_to_all(spectra.astype(jnp.bfloat16), "au", split_axis=0, concat_axis=0, tiled=True),
        "vert",
        split_axis=1,
        concat_axis=1,
        tiled=True,
    ).astype(spectra.dtype)
    whole_rows = arrived.reshape(device_count, 2, block_rows, block_rows)
    third_pass = complex_einsum("jkl,qj->qkl", (whole_rows[:, 0], whole_rows[:, 1]), long_table)
    twist_rows = unit_table(device_count, block_rows, G)
    third_pass = complex_product(third_pass, (twist_rows[0][:, None, :], twist_rows[1][:, None, :]))
    fourth_pass = complex_einsum("qkl,pl->kpq", third_pass, short_table)
    image_scale = 1.0 / (SUB * math.sqrt(own_count * device_count))
    dirty_image = jnp.stack(fourth_pass, axis=1).reshape(block_rows, 2, G) * image_scale
    return (uv_tile, dirty_image)


def solution(mesh):
    return jax.shard_map(
        on_device,
        mesh=mesh,
        in_specs=(
            P(("au", "vert"), None, None),
            P(("au", "vert"), None, None),
            P(),
            P(("au", "vert")),
            P(("au", "vert"), None),
            P(("au", "vert"), None),
            P(("au", "vert"), None, None),
        ),
        out_specs=(P("au", None, "vert"), P(("au", "vert"), None, None)),
        check_vma=False,
    )
```

profile of v0, /device:TPU:1, one launch (start us, length us, event | category | flops | bytes accessed | tf_op | source)
XLA Modules:
  0.0 559.0 jit_solution(18145819555831487277)
XLA Ops:
  10.6 16.7 %all-to-all-start = ((s32[32,2,2]{1,2,0:T(2,128)}), s32[32,2,2]{1,2,0:T(2,128)S(1)}, u32[]{:S(2)}, u32[]{:S(2)}) async-start(s32[32,2,2]{1,2,0:T(2,128)} %copy.49), calls=%async_computation | async-start | bytes 65536 | tf_op jit(solution)/shard_map/all_to_all | solution.py:192
  28.9 185.3 %all-gather.2.cloned.1.call-done = bf16[512,2,1024]{2,1,0:T(2,128)(2,1)} async-done(((bf16[1,2,1024]{2,1,0:T(2,128)(2,1)}), bf16[512,2,1024]{2,1,0:T(2,128)(2,1)}) %all-gather.2.cloned.1.call-update) | async-done | bytes 2097168 | tf_op jit(solution)/shard_map/all_gather | solution.py:161
  214.1 2.3 gather_fusion
  216.5 2.3 gather_fusion.1
  219.1 119.9 %while.15 = (s32[]{:T(128)}, bf16[6,4,2048]{2,1,0:T(4,128)(2,1)S(1)}, bf16[6,4,2,2048]{3,2,1,0:T(2,128)(2,1)}, f32[6,4,2,128]{3,2,1,0:T(2,128)}, f32[16]{0:T(128...) while((s32[]{:T(128)}, ...), condition=%wide.region_2.4_spmd, body=%wide.region_1.3_spmd.sunk | while | flops 94977376 | bytes 7133457 | solution.py:122
  222.0 8.0 %fusion.347 = (bf16[4,32,2048]{2,1,0:T(8,128)(2,1)S(1)}, bf16[4,32,2048]{2,1,0:T(8,128)(2,1)S(1)}, bf16[4,32,2048]{2,1,0:T(8,128)(2,1)S(1)}, bf16[4,32,2048]{2,1,0:T(8,128)(2,1)S(1)}) fusion(f32[4,2048]{1,0:T(4,128)S(1)} %get-tuple-element.319, f32[4,2048]{1,0:T(4,128)S(1)} %get-tuple-element.322, f32[32]{0:T(128)S(1)} %fusion.346, ...), kind=kLoop, calls=%fused_computation.30.clone.1 | loop fusion | flops 3145728 | bytes 2228352 | tf_op jit(solution)/shard_map/while/body/eval_jaxpr/convert_element_type | solution.py:74
  230.0 3.6 fusion.348
  242.0 8.0 %fusion.347 = (bf16[4,32,2048]{2,1,0:T(8,128)(2,1)S(1)}, bf16[4,32,2048]{2,1,0:T(8,128)(2,1)S(1)}, bf16[4,32,2048]{2,1,0:T(8,128)(2,1)S(1)}, bf16[4,32,2048]{2,1,0:T(8,128)(2,1)S(1)}) fusion(f32[4,2048]{1,0:T(4,128)S(1)} %get-tuple-element.319, f32[4,2048]{1,0:T(4,128)S(1)} %get-tuple-element.322, f32[32]{0:T(128)S(1)} %fusion.346, ...), kind=kLoop, calls=%fused_computation.30.clone.1 | loop fusion | flops 3145728 | bytes 2228352 | tf_op jit(solution)/shard_map/while/body/eval_jaxpr/convert_element_type | solution.py:74
  250.0 3.6 fusion.348
  262.0 8.0 %fusion.347 = (bf16[4,32,2048]{2,1,0:T(8,128)(2,1)S(1)}, bf16[4,32,2048]{2,1,0:T(8,128)(2,1)S(1)}, bf16[4,32,2048]{2,1,0:T(8,128)(2,1)S(1)}, bf16[4,32,2048]{2,1,0:T(8,128)(2,1)S(1)}) fusion(f32[4,2048]{1,0:T(4,128)S(1)} %get-tuple-element.319, f32[4,2048]{1,0:T(4,128)S(1)} %get-tuple-element.322, f32[32]{0:T(128)S(1)} %fusion.346, ...), kind=kLoop, calls=%fused_computation.30.clone.1 | loop fusion | flops 3145728 | bytes 2228352 | tf_op jit(solution)/shard_map/while/body/eval_jaxpr/convert_element_type | solution.py:74
  270.0 3.6 fusion.348
  282.0 8.0 %fusion.347 = (bf16[4,32,2048]{2,1,0:T(8,128)(2,1)S(1)}, bf16[4,32,2048]{2,1,0:T(8,128)(2,1)S(1)}, bf16[4,32,2048]{2,1,0:T(8,128)(2,1)S(1)}, bf16[4,32,2048]{2,1,0:T(8,128)(2,1)S(1)}) fusion(f32[4,2048]{1,0:T(4,128)S(1)} %get-tuple-element.319, f32[4,2048]{1,0:T(4,128)S(1)} %get-tuple-element.322, f32[32]{0:T(128)S(1)} %fusion.346, ...), kind=kLoop, calls=%fused_computation.30.clone.1 | loop fusion | flops 3145728 | bytes 2228352 | tf_op jit(solution)/shard_map/while/body/eval_jaxpr/convert_element_type | solution.py:74
  289.9 3.6 fusion.348
  301.9 8.0 %fusion.347 = (bf16[4,32,2048]{2,1,0:T(8,128)(2,1)S(1)}, bf16[4,32,2048]{2,1,0:T(8,128)(2,1)S(1)}, bf16[4,32,2048]{2,1,0:T(8,128)(2,1)S(1)}, bf16[4,32,2048]{2,1,0:T(8,128)(2,1)S(1)}) fusion(f32[4,2048]{1,0:T(4,128)S(1)} %get-tuple-element.319, f32[4,2048]{1,0:T(4,128)S(1)} %get-tuple-element.322, f32[32]{0:T(128)S(1)} %fusion.346, ...), kind=kLoop, calls=%fused_computation.30.clone.1 | loop fusion | flops 3145728 | bytes 2228352 | tf_op jit(solution)/shard_map/while/body/eval_jaxpr/convert_element_type | solution.py:74
  309.9 3.6 fusion.348
  321.9 8.0 %fusion.347 = (bf16[4,32,2048]{2,1,0:T(8,128)(2,1)S(1)}, bf16[4,32,2048]{2,1,0:T(8,128)(2,1)S(1)}, bf16[4,32,2048]{2,1,0:T(8,128)(2,1)S(1)}, bf16[4,32,2048]{2,1,0:T(8,128)(2,1)S(1)}) fusion(f32[4,2048]{1,0:T(4,128)S(1)} %get-tuple-element.319, f32[4,2048]{1,0:T(4,128)S(1)} %get-tuple-element.322, f32[32]{0:T(128)S(1)} %fusion.346, ...), kind=kLoop, calls=%fused_computation.30.clone.1 | loop fusion | flops 3145728 | bytes 2228352 | tf_op jit(solution)/shard_map/while/body/eval_jaxpr/convert_element_type | solution.py:74
  329.9 3.6 fusion.348
  339.2 0.9 reshape.466
  340.1 7.4 %all-to-all-start.1 = ((bf16[32,2,2048]{2,1,0:T(2,128)(2,1)}), bf16[32,2,2048]{2,1,0:T(2,128)(2,1)S(1)}, u32[]{:S(2)}, u32[]{:S(2)}) async-start(bf16[32,2,2048]{2,1,0:T(2,128)(2,1)} %reshape.466), calls=%async_computation.1 | async-start | bytes 524288 | tf_op jit(solution)/shard_map/all_to_all | solution.py:191
  347.9 21.8 %all-to-all-done.1 = bf16[32,2,2048]{2,1,0:T(2,128)(2,1)S(1)} async-done(((bf16[32,2,2048]{2,1,0:T(2,128)(2,1)}), bf16[32,2,2048]{2,1,0:T(2,128)(2,1)S(1)}, u32[]{:S(2)}, u32[]{:S(2)}) %all-to-all-start.1) | async-done | bytes 262176 | tf_op jit(solution)/shard_map/all_to_all | solution.py:191
  370.2 1.0 convolution_bitcast_fusion
  371.2 3.9 copy.56
  375.1 2.4 copy.81
  377.5 13.5 %scatter_custom_fusion = f32[544,512]{1,0:T(8,128)S(1)} fusion(s32[2048]{0:T(1024)S(1)} %reshape.493, f32[2048,512]{1,0:T(8,128)} %bitcast.254, f32[]{:T(128)} %constant.250.clone.1), kind=kCustom, calls=%fused_computation.192 | custom fusion | flops 1048576 | bytes 1114624 | tf_op jit(solution)/shard_map/scatter-add | solution.py:145
  391.0 3.2 collective-permute-start
  394.2 1.0 slice.178
  395.2 3.7 collective-permute-done
  399.6 1.9 reshape.468
  401.5 1.2 convert_element_type.204
  402.7 5.8 %all-to-all-start.2 = ((bf16[512,2,256]{2,1,0:T(2,128)(2,1)}), bf16[512,2,256]{2,1,0:T(2,128)(2,1)S(1)}, u32[]{:S(2)}, u32[]{:S(2)}) async-start(bf16[512,2,256]{2,1,0:T(2,128)(2,1)} %convert_element_type.204), calls=%async_computation.2 | async-start | bytes 1048576 | tf_op jit(solution)/shard_map/all_to_all | solution.py:203
  408.6 33.0 %all-to-all-done.2 = bf16[512,2,256]{2,1,0:T(2,128)(2,1)S(1)} async-done(((bf16[512,2,256]{2,1,0:T(2,128)(2,1)}), bf16[512,2,256]{2,1,0:T(2,128)(2,1)S(1)}, u32[]{:S(2)}, u32[]{:S(2)}) %all-to-all-start.2) | async-done | bytes 524320 | tf_op jit(solution)/shard_map/all_to_all | solution.py:203
  443.7 5.0 fusion.135
  448.7 5.2 fusion.131
  453.9 5.0 fusion.126
  459.7 0.8 copy.60
  460.5 5.2 fusion.125
  466.5 0.8 copy.61
  467.4 13.5 %all_to_all.35 = bf16[16,32,2,256]{3,1,2,0:T(8,128)(2,1)S(1)} all-to-all(bf16[16,32,2,256]{3,1,2,0:T(8,128)(2,1)S(1)} %pad_maximum_fusion.1), channel_id=1, replica_groups=mesh['au'=16,'vert'=32] {'au'}, dimensions={0} | all-to-all | bytes 1048576 | tf_op jit(solution)/shard_map/all_to_all | solution.py:217
  480.9 1.1 copy.62
  482.0 5.4 all-to-all-start.4
  487.6 33.4 %all-to-all-done.4 = bf16[16,32,2,256]{3,0,2,1:T(8,128)(2,1)S(1)} async-done(((bf16[16,32,2,256]{3,0,2,1:T(8,128)(2,1)}), bf16[16,32,2,256]{3,0,2,1:T(8,128)(2,1)S(1)}, u32[]{:S(2)}, u32[]{:S(2)}) %all-to-all-start.4) | async-done | bytes 524320 | tf_op jit(solution)/shard_map/all_to_all | solution.py:216
  520.9 2.2 copy.63
  523.1 2.1 reshape.470
  525.2 5.0 fusion.150
  530.3 5.1 fusion.158
  535.3 5.1 fusion.156
  540.4 5.3 fusion.152
  549.7 2.1 maximum_multiply_fusion
  (283 shorter events, 64.0 us)
Async XLA Ops:
  7.2 206.9 %all-gather.2.cloned.1.call-start = ((), (), s32[]{:S(2)}) async-start(), calls=%async_computation.5 | async-start | bytes 2101248 | tf_op jit(solution)/shard_map/all_gather | solution.py:161
  10.6 329.5 %all-to-all-start = ((s32[32,2,2]{1,2,0:T(2,128)}), s32[32,2,2]{1,2,0:T(2,128)S(1)}, u32[]{:S(2)}, u32[]{:S(2)}) async-start(s32[32,2,2]{1,2,0:T(2,128)} %copy.49), calls=%async_computation | async-start | bytes 65536 | tf_op jit(solution)/shard_map/all_to_all | solution.py:192
  340.1 29.5 %all-to-all-start.1 = ((bf16[32,2,2048]{2,1,0:T(2,128)(2,1)}), bf16[32,2,2048]{2,1,0:T(2,128)(2,1)S(1)}, u32[]{:S(2)}, u32[]{:S(2)}) async-start(bf16[32,2,2048]{2,1,0:T(2,128)(2,1)} %reshape.466), calls=%async_computation.1 | async-start | bytes 524288 | tf_op jit(solution)/shard_map/all_to_all | solution.py:191
  391.0 8.0 %collective-permute-start = (bf16[32,512]{1,0:T(8,128)(2,1)S(1)}, bf16[32,512]{1,0:T(8,128)(2,1)S(1)}, u32[]{:S(2)}, u32[]{:S(2)}) collective-permute-start(bf16[32,512]{1,0:T(8,128)(2,1)S(1)} %slice.226), channel_id=1, source_target_pairs={{0,32},{32,64},{64,96},{96,128},{128,160},{160,192},{192,224},{224... | collective-permute-start | bytes 98312 | tf_op jit(solution)/shard_map/ppermute | solution.py:19
  401.5 40.5 %copy-start = (f32[512,2,256]{2,1,0:T(2,128)}, f32[512,2,256]{2,1,0:T(2,128)S(1)}, u32[]{:S(2)}) copy-start(f32[512,2,256]{2,1,0:T(2,128)S(1)} %reshape.468) | copy-start | bytes 3145732
  402.7 38.9 %all-to-all-start.2 = ((bf16[512,2,256]{2,1,0:T(2,128)(2,1)}), bf16[512,2,256]{2,1,0:T(2,128)(2,1)S(1)}, u32[]{:S(2)}, u32[]{:S(2)}) async-start(bf16[512,2,256]{2,1,0:T(2,128)(2,1)} %convert_element_type.204), calls=%async_computation.2 | async-start | bytes 1048576 | tf_op jit(solution)/shard_map/all_to_all | solution.py:203
  482.0 39.0 %all-to-all-start.4 = ((bf16[16,32,2,256]{3,0,2,1:T(8,128)(2,1)}), bf16[16,32,2,256]{3,0,2,1:T(8,128)(2,1)S(1)}, u32[]{:S(2)}, u32[]{:S(2)}) async-start(bf16[16,32,2,256]{3,0,2,1:T(8,128)(2,1)} %copy.62), calls=%async_computation.4 | async-start | bytes 1048576 | tf_op jit(solution)/shard_map/all_to_all | solution.py:216
Sparse Core Ops, SparseCore 0:
  12.6 201.5 all-gather.1
where the time goes:
time: 568 us; the launch traced here: 559 us
  waiting for transfers between devices  278 us (49%)
  other arithmetic  92.1 us (16%)
  matrix products  74.3 us (13%)
  local copies, waits for them, and re-layouts  46.4 us (8%)
  starting transfers between devices  38.5 us (7%)
  between operations  14.9 us (3%)
  blocking collectives  13.5 us (2%)
    all_gather x1, waiting for transfers between devices, on_device(): beam_table = lax.all_gather(beam_terms, ('au', 'vert'), axis=0, tiled=True)  185 us
    convert_element_type x6, other arithmetic, grid_subgrids(): weighted_re = (vis_re * cos_u - vis_im * sin_u).astype(jnp.bfloat16)  47.8 us
    all_to_all x1, waiting for transfers between devices, on_device(): lax.all_to_all(lax.all_to_all(spectra.astype(jnp.bfloat16), 'au', split_a...  33.4 us
    all_to_all x1, waiting for transfers between devices, on_device(): lax.all_to_all(uv_tile.astype(jnp.bfloat16), 'vert', split_axis=0, concat...  33 us
    all_to_all x1, waiting for transfers between devices, on_device(): lax.all_to_all(uv_send, 'vert', split_axis=0, concat_axis=0, tiled=True)  21.8 us
    neg x6, other arithmetic, grid_subgrids(): -phasor_im  21.6 us
    unnamed x4, matrix products  20.4 us
    all_to_all x1, starting transfers between devices, on_device(): lax.all_to_all(offset_send, 'vert', split_axis=0, concat_axis=0, tiled=True)  16.7 us
  transfers between devices with their start and end apart: 6, of which 5 were waited for; matrix products, arithmetic and copies ran while one was open for 23% of the time, Pallas kernels for 0%

commit v1 on v0

v1 whole, which is shorter than its diff:
```python
import math
import numpy as np
import jax
import jax.numpy as jnp
from jax import lax
from jax.experimental import pallas as pl
from jax.experimental.pallas import tpu as pltpu

SUB = 32
NS = 24
NK = 2048
F32 = jnp.float32
BF = jnp.bfloat16
VM = pl.BlockSpec(memory_space=pltpu.VMEM)
SM = pl.BlockSpec(memory_space=pltpu.SMEM)


def cmul(ar, ai, br, bi):
    return ar * br - ai * bi, ar * bi + ai * br


def base_phase(theta):
    t = theta * theta
    s = F32(0.0)
    for n in range(17, 1, -2):
        s = (s + F32((-1.0) ** ((n - 1) // 2) / math.factorial(n))) * t
    c = F32(0.0)
    for n in range(18, 0, -2):
        c = (c + F32((-1.0) ** (n // 2) / math.factorial(n))) * t
    return c + F32(1.0), theta * (s + F32(1.0))


def sky_kernel(vis_ref, off_ref, scale_ref, sky_ref, zu, mu, zv, wp):
    time_id = lax.broadcasted_iota(jnp.int32, (128, NK), 0)
    k_id = lax.broadcasted_iota(jnp.int32, (128, NK), 1)
    spread = (lax.shift_right_logical(k_id, 4) == time_id).astype(F32)
    scale = scale_ref[...] * F32(2.0 * math.pi / SUB)
    def put(dest, n, pair):
        for part in range(2):
            for lo in range(0, NK, 128):
                dest[n + part, lo // 128, 0:NS, :] = pair[part][:, lo:lo + 128]

    for axis in range(2):
        shift = jnp.dot(off_ref[axis], spread, precision=lax.Precision.HIGHEST, preferred_element_type=F32)
        e1 = base_phase(shift * scale)
        e2 = cmul(*e1, *e1)
        e4 = cmul(*e2, *e2)
        e8 = cmul(*e4, *e4)
        e16 = cmul(*e8, *e8)
        dest = (zu, zv)[axis]
        put(dest, 0, e1)
        put(dest, 2, e2)
        put(dest, 4, e4)
        if axis == 1:
            put(zv, 6, e8)
            put(zv, 8, e16)
        else:
            vis = vis_ref[0], vis_ref[1]
            put(mu, 0, cmul(*vis, e16[0], -e16[1]))
            put(mu, 2, cmul(*vis, e8[0], -e8[1]))
            put(mu, 4, vis)
            put(mu, 6, cmul(*vis, *e8))

    row = lax.broadcasted_iota(jnp.int32, (8, 128), 0)
    bit0, bit1, bit2 = [(lax.shift_right_logical(row, n) & 1) == 1 for n in range(3)]
    one = jnp.ones((8, 128), F32)
    zero = jnp.zeros((8, 128), F32)

    def wide(ref, n, s, lo):
        return ref[n, lo // 128, pl.ds(s, 8, stride=0), :]

    def base_tile(ref, s, lo):
        tr = jnp.where(bit0, wide(ref, 0, s, lo), one)
        ti = jnp.where(bit0, wide(ref, 1, s, lo), zero)
        tr, ti = cmul(tr, ti, jnp.where(bit1, wide(ref, 2, s, lo), one), jnp.where(bit1, wide(ref, 3, s, lo), zero))
        return cmul(tr, ti, jnp.where(bit2, wide(ref, 4, s, lo), one), jnp.where(bit2, wide(ref, 5, s, lo), zero))

    def one_subgrid(s, slot):
        for lo in range(0, NK, 128):
            br, bi = base_tile(zu, s, lo)
            blocks = [cmul(br, bi, wide(mu, 2 * n, s, lo), wide(mu, 2 * n + 1, s, lo)) for n in range(4)]
            for part in range(2):
                for half in range(2):
                    wp[slot, part * 32 + half * 16:part * 32 + half * 16 + 16, lo:lo + 128] = jnp.concatenate(
                        [blocks[2 * half][part], blocks[2 * half + 1][part]], axis=0).astype(BF)
            br, bi = base_tile(zv, s, lo)
            e8r, e8i = wide(zv, 6, s, lo), wide(zv, 7, s, lo)
            e16r, e16i = wide(zv, 8, s, lo), wide(zv, 9, s, lo)
            blocks = [cmul(br, bi, e16r, -e16i), cmul(br, bi, e8r, -e8i), (br, bi), cmul(br, bi, e8r, e8i)]
            for part in range(2):
                for half in range(2):
                    wp[slot, 64 + part * 32 + half * 16:64 + part * 32 + half * 16 + 16, lo:lo + 128] = jnp.concatenate(
                        [blocks[2 * half][part], blocks[2 * half + 1][part]], axis=0).astype(BF)

    def finish(s, slot):
        prod = lax.dot_general(wp[slot, 0:64, :], wp[slot, 64:128, :], (((1,), (1,)), ((), ())), preferred_element_type=F32)
        sky_ref[s, 0:32, :] = prod[0:32, 0:32] - prod[32:64, 32:64]
        sky_ref[s, 32:64, :] = prod[0:32, 32:64] + prod[32:64, 0:32]

    def pair(i, _):
        one_subgrid(2 * i, 0)
        one_subgrid(2 * i + 1, 1)
        finish(2 * i, 0)
        finish(2 * i + 1, 1)
        return 0

    lax.fori_loop(0, NS // 2, pair, 0)


def sky_call(vis, off, scale):
    return pl.pallas_call(
        sky_kernel,
        out_shape=jax.ShapeDtypeStruct((NS, 64, 32), F32),
        in_specs=[VM] * 3, out_specs=VM,
        scratch_shapes=[pltpu.VMEM((6, 16, 32, 128), F32), pltpu.VMEM((8, 16, 32, 128), F32), pltpu.VMEM((10, 16, 32, 128), F32),
                        pltpu.VMEM((2, 128, NK), BF)],
        name="sky",
        cost_estimate=pl.CostEstimate(flops=24 * 64 * 64 * 2048 * 2 * 20, bytes_accessed=4 << 20, transcendentals=0),
    )(vis, off, scale)


def dft_tables():
    x = np.arange(32) - 16
    phi = 2.0 * np.pi / 32 * (x[:, None] * x[None, :] % 32)
    c, s = np.cos(phi) / 32, np.sin(phi) / 32
    left = np.block([[c, s], [-s, c]])
    right = np.concatenate([c, s], axis=1)
    return left.astype(np.float32), right.astype(np.float32)


def uv_kernel(st_ref, ints_ref, depth_ref, sky_ref, beam_ref, meta_ref, left_ref, right_ref, rows_ref, slot_ref, mr_ref, g_ref, rb_ref):
    x = lax.broadcasted_iota(jnp.int32, (8, 128), 0)
    lane = lax.broadcasted_iota(jnp.int32, (8, 128), 1)
    p = 4 * x + lax.shift_right_logical(lane, 5) - 16
    q = (lane & 31) - 16
    pf, qf = p.astype(F32), q.astype(F32)
    ap, aq = pf * F32(0.1 / 32), qf * F32(0.1 / 32)
    rad = ap * ap + aq * aq
    tp = (2.0 * pf + 1.0) * F32(1.0 / 32)
    tq = (2.0 * qf + 1.0) * F32(1.0 / 32)
    taper = (1.0 - tp * tp) * (1.0 - tq * tq) * F32(1.0 / math.sqrt(NK))

    def one(s, _):
        a = beam_ref[st_ref[s, 0]].astype(F32)
        b = beam_ref[st_ref[s, 1]].astype(F32)
        pr = a[0:8] * b[0:8] + a[8:16] * b[8:16]
        pi_ = a[8:16] * b[0:8] - a[0:8] * b[8:16]
        turn = (ints_ref[0, s] * p + ints_ref[1, s] * q) & 31
        ang = turn.astype(F32) * F32(2.0 * math.pi / 32) - F32(math.pi) * depth_ref[s] * rad
        sc, ss = jnp.cos(ang) * taper, jnp.sin(ang) * taper
        mr, mi = cmul(pr, pi_, sc, ss)
        for y in range(4):
            ra = mr if y == 0 else pltpu.roll(mr, 128 - 32 * y, 1)
            rb = mi if y == 0 else pltpu.roll(mi, 128 - 32 * y, 1)
            mr_ref[pl.ds(y, 8, stride=4), :] = ra
            mr_ref[pl.ds(32 + y, 8, stride=4), :] = rb
        kr, ki = mr_ref[0:32, 0:32], mr_ref[32:64, 0:32]
        sr, si = sky_ref[s, 0:32, :], sky_ref[s, 32:64, :]
        cr, ci = cmul(sr, si, kr, ki)
        cor = jnp.concatenate([cr, ci], axis=0).astype(BF)
        g = jnp.dot(left_ref[...], cor, preferred_element_type=F32)
        g_ref[pl.ds(pl.multiple_of(s * 64, 64), 64), :] = g.astype(BF)
        return 0

    lax.fori_loop(0, NS, one, 0, unroll=2)

    slot_ref[...] = jnp.zeros_like(slot_ref)
    wide_lane = lax.broadcasted_iota(jnp.int32, (32, 128), 1)
    note_lane = lax.broadcasted_iota(jnp.int32, (16, 128), 1)

    def two(y, _):
        outs = []
        for half in range(2):
            s = y + 12 * half
            yv = jnp.dot(g_ref[pl.ds(pl.multiple_of(s * 64, 64), 64), :], right_ref[...], preferred_element_type=F32)
            re = yv[0:32, 0:32] + yv[32:64, 32:64]
            im = yv[32:64, 0:32] - yv[0:32, 32:64]
            both = jnp.concatenate([re, im], axis=1)
            outs.append(both)
            dest, rank = ints_ref[2, s], ints_ref[3, s]
            mine = lax.shift_right_logical(wide_lane, 6) == rank
            held = slot_ref[dest, 0:32, :].astype(F32)
            slot_ref[dest, 0:32, :] = jnp.where(mine, jnp.concatenate([both, both], axis=1), held).astype(BF)
            notes = slot_ref[dest, 32:48, :].astype(F32)
            for n in range(3):
                notes = jnp.where(note_lane == rank * 64 + n, ints_ref[4 + n, s].astype(F32), notes)
            slot_ref[dest, 32:48, :] = notes.astype(BF)
        rb_ref[pl.ds(y, 32, stride=16), :] = jnp.concatenate(outs, axis=1)
        return 0

    lax.fori_loop(0, 12, two, 0)
    for n in range(4):
        rb_ref[pl.ds(12 + n, 32, stride=16), :] = jnp.broadcast_to(meta_ref[n:n + 1, :], (32, 128))
    rows_ref[...] = rb_ref[...].astype(BF)


def uv_call(stations, ints, depth, sky, beam, meta):
    left, right = dft_tables()
    return pl.pallas_call(
        uv_kernel,
        out_shape=(jax.ShapeDtypeStruct((512, 128), BF), jax.ShapeDtypeStruct((32, 48, 128), BF)),
        in_specs=[SM] * 3 + [VM] * 5, out_specs=(VM, VM),
        scratch_shapes=[pltpu.VMEM((64, 128), F32), pltpu.VMEM((NS * 64, 32), BF), pltpu.VMEM((512, 128), F32)],
        name="uv",
    )(stations, ints, depth, sky, beam, meta, jnp.asarray(left, BF), jnp.asarray(right, BF))


def phase_table(rows, cols, period):
    phi = 2.0 * np.pi / period * (np.arange(rows)[:, None] * np.arange(cols)[None, :] % period)
    return np.cos(phi), np.sin(phi)


NG = 17
MSG = 48


def row_kernel(me_ref, recv_ref, stage1_ref, twist_ref, stage2_ref, out_ref, scr, lhs, oht, yv, buf):
    scr[...] = recv_ref[...].astype(F32)
    lane = lax.broadcasted_iota(jnp.int32, (32, 768), 1)
    src = lax.broadcasted_iota(jnp.int32, (32, 768), 0)
    pick_src = ((lane & 31) == src).astype(BF)
    pick_item = lax.shift_right_logical(lane, 5) == src

    def meta(n):
        table = jnp.transpose(scr[pl.ds(12 + n, 32, stride=16), :])[0:32]
        spread = jnp.dot(table.astype(BF), pick_src, preferred_element_type=F32)
        return jnp.sum(jnp.where(pick_item, spread, 0.0), axis=0, keepdims=True)

    g_hi, g_lo, h, e = [meta(n) for n in range(4)]
    me = me_ref[0].astype(F32)
    g = g_hi + jnp.where(g_lo > me, 1.0, 0.0)
    h_id = lax.broadcasted_iota(jnp.int32, (256, 768), 0).astype(F32)
    oht[:, 0:768] = (h_id == h).astype(BF)
    oht[:, 768:1536] = (h_id == h + 1.0).astype(BF)
    col = (lax.broadcasted_iota(jnp.int32, (64, 384), 0) & 31).astype(F32)
    for half in range(2):
        parts = []
        for blk in range(3):
            rows = jnp.concatenate([scr[pl.ds(4 * blk + n, 32, stride=16), :] for n in range(4)], axis=0)
            parts.append(jnp.transpose(rows)[half * 64:half * 64 + 64])
        v = jnp.concatenate(parts, axis=1)
        at = half * 384
        first = col >= e[:, at:at + 384]
        hi = jnp.where(first, v, 0.0)
        lo = jnp.where(first, 0.0, v)
        for n in range(NG):
            here = g[:, at:at + 384] == float(n)
            lhs[n * 64:n * 64 + 64, at:at + 384] = jnp.where(here, hi, 0.0).astype(BF)
            lhs[n * 64:n * 64 + 64, 768 + at:768 + at + 384] = jnp.where(here, lo, 0.0).astype(BF)
    x = lax.dot_general(lhs[...], oht[...], (((1,), (1,)), ((), ())), preferred_element_type=F32).astype(BF)
    yv[...] = jnp.dot(x, stage1_ref[...], preferred_element_type=F32)
    for n in range(NG):
        y = yv[n * 64:n * 64 + 64, :]
        re = y[0:32, 0:256] - y[32:64, 256:512]
        im = y[0:32, 256:512] + y[32:64, 0:256]
        re, im = cmul(re, im, twist_ref[0], twist_ref[1])
        z = jnp.dot(stage2_ref[...], jnp.concatenate([re, im], axis=0).astype(BF), preferred_element_type=F32)
        for low in range(2):
            for comp in range(2):
                row = comp * 16 + n if n < 16 else 32 + comp
                for k in range(2):
                    at = (low * 2 + comp) * 16
                    buf[low * 2 + k, pl.ds(row, 16, stride=MSG), :] = z[at:at + 16, k * 128:k * 128 + 128]
    for k in range(4):
        out_ref[:, k * 128:k * 128 + 128] = buf[k].astype(BF)


def row_tables():
    c, s = phase_table(256, 256, 256)
    stage1 = np.concatenate([c, s], axis=1)
    twist = np.stack(phase_table(32, 256, 8192))
    c, s = phase_table(32, 32, 32)
    full = np.stack([np.concatenate([c, -s], axis=1), np.concatenate([s, c], axis=1)])
    stage2 = full.reshape(2, 16, 2, 64).transpose(2, 0, 1, 3).reshape(64, 64)
    return stage1, twist, stage2


def row_call(me, recv):
    stage1, twist, stage2 = row_tables()
    return pl.pallas_call(
        row_kernel,
        out_shape=jax.ShapeDtypeStruct((16 * MSG, 512), BF),
        in_specs=[SM] + [VM] * 4, out_specs=VM,
        scratch_shapes=[pltpu.VMEM((512, 128), F32), pltpu.VMEM((NG * 64, 1536), BF), pltpu.VMEM((256, 1536), BF),
                        pltpu.VMEM((NG * 64, 512), F32), pltpu.VMEM((4, 16 * MSG, 128), F32)],
        name="rows",
    )(me, recv, jnp.asarray(stage1, BF), jnp.asarray(twist, F32), jnp.asarray(stage2, BF))


def high_kernel(me_ref, recv_ref, table_ref, out_ref, xh):
    first = lax.broadcasted_iota(jnp.int32, (16, 512), 0) == 0
    for r in range(16):
        for comp in range(2):
            block = recv_ref[r * MSG + comp * 16:r * MSG + comp * 16 + 16, :].astype(F32)
            before = ((r + 15) % 16) * MSG + 32
            spill = recv_ref[before:before + 16, :].astype(F32)[comp:comp + 1]
            xh[comp * 256 + r * 16:comp * 256 + r * 16 + 16, :] = jnp.where(first, block + spill, block).astype(BF)
    y = lax.dot_general(xh[...], table_ref[...], (((0,), (0,)), ((), ())), preferred_element_type=F32)
    ql = lax.broadcasted_iota(jnp.int32, (8, 256), 1)
    ang = (ql * me_ref[0]).astype(F32) * F32(2.0 * math.pi / 8192)
    re, im = cmul(y[:, 0:256], y[:, 256:512], jnp.cos(ang)[0:1], jnp.sin(ang)[0:1])
    out_ref[:, 0:256] = re.astype(BF)
    out_ref[:, 256:512] = im.astype(BF)


def high_call(me, recv):
    c, s = phase_table(256, 256, 256)
    table = np.block([[c, s], [-s, c]])
    return pl.pallas_call(
        high_kernel,
        out_shape=jax.ShapeDtypeStruct((512, 512), BF),
        in_specs=[SM] + [VM] * 2, out_specs=VM,
        scratch_shapes=[pltpu.VMEM((512, 512), BF)],
        name="high",
    )(me, recv, jnp.asarray(table, BF))


def low_kernel(recv_ref, table_ref, out_ref, scr):
    for k in range(4):
        scr[k] = recv_ref[:, k * 128:k * 128 + 128].astype(F32)
    for m in range(16):
        parts = [jnp.concatenate([scr[2 * comp + k, pl.ds(m, 32, stride=16), :] for k in range(2)], axis=1) for comp in range(2)]
        x = jnp.concatenate(parts, axis=0).astype(BF)
        out_ref[m] = jnp.dot(table_ref[...], x, preferred_element_type=F32) * F32(1.0 / (SUB * math.sqrt(12288)))


def low_call(recv):
    c, s = phase_table(32, 32, 32)
    table = np.block([[c, -s], [s, c]])
    return pl.pallas_call(
        low_kernel,
        out_shape=jax.ShapeDtypeStruct((16, 64, 256), F32),
        in_specs=[VM] * 2, out_specs=VM,
        scratch_shapes=[pltpu.VMEM((4, 512, 128), F32)],
        name="low",
    )(recv, jnp.asarray(table, BF))


def tile_kernel(notes_ref, recv_ref, rep_ref, acc_ref):
    acc_ref[...] = jnp.zeros_like(acc_ref)
    row = lax.broadcasted_iota(jnp.int32, (32, 256), 0)
    column = lax.broadcasted_iota(jnp.int32, (32, 256), 1)

    def one(n, _):
        wide = jnp.dot(recv_ref[n, 0:32, :], rep_ref[...], preferred_element_type=F32)
        for rank in range(2):
            hi, lo, start = [notes_ref[n, rank * 3 + k] for k in range(3)]
            seen = (column >= start) & (column < start + 32)
            upper = seen & (row >= lo)
            lower = seen & (row < lo)
            for comp in range(2):
                x = wide[:, (rank * 2 + comp) * 256:(rank * 2 + comp) * 256 + 256]
                acc_ref[hi, comp] += jnp.where(upper, x, 0.0)
                acc_ref[hi + 1, comp] += jnp.where(lower, x, 0.0)
        return 0

    lax.fori_loop(0, 32, one, 0)


def tile_call(notes, recv):
    rep = np.zeros((128, 1024), np.float32)
    for part in range(4):
        for v in range(256):
            rep[part * 32 + v % 32, part * 256 + v] = 1.0
    return pl.pallas_call(
        tile_kernel,
        out_shape=jax.ShapeDtypeStruct((NG, 2, 32, 256), F32),
        in_specs=[SM] + [VM] * 2, out_specs=VM,
        name="tile",
    )(notes, recv, jnp.asarray(rep, BF))


def gather_beams(beam_terms):
    table = lax.all_gather(beam_terms.reshape(1, 16, 128), "vert", axis=0, tiled=True)
    return lax.all_gather(table, "au", axis=0, tiled=True)


def exchange(value, axis, parts):
    rows, cols = value.shape
    return lax.all_to_all(value.reshape(parts, rows // parts, cols), axis, split_axis=0, concat_axis=0, tiled=True).reshape(rows, cols)


def on_device(visibilities, baseline_offsets, channel_scale, screen_depth, stations, corners, beam_terms):
    au, vert = lax.axis_index("au"), lax.axis_index("vert")
    me = vert.astype(jnp.int32).reshape(1)
    beams = gather_beams(beam_terms)
    row, col = corners[:, 0], corners[:, 1]
    dest = col // 256
    order = jnp.arange(NS, dtype=jnp.int32)
    rank = jnp.sum(((dest[None, :] == dest[:, None]) & (order[None, :] < order[:, None])).astype(jnp.int32), axis=1)
    hi, lo = (row - au * 512) // 32, row % 32
    ints = jnp.stack([row, col, dest, rank, hi, lo, col % 256])
    meta = jnp.pad(jnp.stack([hi, lo, col // 32, col % 32]).astype(F32), ((0, 0), (0, 128 - NS)))
    sky = sky_call(
        visibilities.transpose(1, 0, 2).astype(F32),
        baseline_offsets.transpose(1, 0, 2),
        jnp.broadcast_to(channel_scale[None, :], (128, 16)).reshape(1, NK),
    )
    rows, slots = uv_call(stations, ints, screen_depth, sky, beams, meta)
    rows = exchange(rows, "vert", 32)
    slots = lax.all_to_all(slots, "vert", split_axis=0, concat_axis=0, tiled=True)
    high_in = exchange(row_call(me, rows), "au", 16)
    low_in = exchange(high_call(me, high_in), "vert", 32)
    dirty = low_call(low_in).reshape(16, 2, 8192)
    notes = slots[:, 32, :]
    notes = jnp.concatenate([notes[:, 0:3], notes[:, 64:67]], axis=1).astype(jnp.int32)
    tile = tile_call(notes, slots)
    spill = lax.ppermute(tile[16].astype(BF), "au", [(n, (n + 1) % 16) for n in range(16)])
    first = tile[0] + spill.astype(F32)
    gridded = jnp.concatenate([first[None], tile[1:16]], axis=0).transpose(0, 2, 1, 3).reshape(512, 2, 256)
    return gridded, dirty


def solution(mesh):
    from jax.sharding import PartitionSpec as P

    both = ("au", "vert")
    return jax.shard_map(
        on_device,
        mesh=mesh,
        in_specs=(P(both, None, None), P(both, None, None), P(), P(both), P(both, None), P(both, None), P(both, None, None)),
        out_specs=(P("au", None, "vert"), P(both, None, None)),
        check_vma=False,
    )
```

time: 568 us -> 252 us (0.44); the launches traced: 559 us -> 251 us
  waiting for transfers between devices: 278 us -> 92.7 us
  other arithmetic: 92.1 us -> 4.95 us
  matrix products: 74.3 us -> 0 us
  blocking collectives: 13.5 us -> 57.8 us
  Pallas kernels: 0 us -> 41 us
  local copies, waits for them, and re-layouts: 46.4 us -> 13.2 us
  starting transfers between devices: 38.5 us -> 27.6 us
    all_gather x1, waiting for transfers between devices: 185 us -> 31.7 us  [gather_beams(): return lax.all_gather(table, 'au', axis=0, tiled=True)]
    dot_general x70 -> x0, matrix products: 53.9 us -> none  [the longest x15 12 us: complex_einsum(): jnp.einsum(formula, left_im, right_re, precision=highest)]
    convert_element_type x19 -> x3, other arithmetic: 49.1 us -> 2.44 us  [the longest x1 1.74 us: on_device(): visibilities.transpose(1, 0, 2).astype(F32)]
    pallas_call x0 -> x6, Pallas kernels: none -> 41 us  [the longest x1 13.3 us: sky_call(): pl.pallas_call(sky_kernel, out_shape=jax.ShapeDtypeStruct((NS, 64, 32), F...]
    all_gather x0 -> x1, blocking collectives: none -> 40.6 us  [gather_beams(): lax.all_gather(beam_terms.reshape(1, 16, 128), 'vert', axis=0, tiled=True)]
    all_to_all x4 -> x3, waiting for transfers between devices: 88.1 us -> 55.1 us  [the longest x2 29.8 us: exchange(): lax.all_to_all(value.reshape(parts, rows // parts, cols), axis, split_axi...]
    neg x6 -> x0, other arithmetic: 21.6 us -> none  [grid_subgrids(): -phasor_im]
    unnamed x4 -> x0, matrix products: 20.4 us -> none
  transfers between devices with their start and end apart: 6 -> 5, of which waited for: 5 -> 5; matrix products, arithmetic and copies ran while one was open for 23% -> 5% of each run, Pallas kernels for 0% -> 9%
where the time goes in v1:
time: 252 us; the launch traced here: 251 us
  waiting for transfers between devices  92.7 us (37%)
  blocking collectives  57.8 us (23%)
  Pallas kernels  41 us (16%)
  starting transfers between devices  27.6 us (11%)
  between operations  14.1 us (6%)
  local copies, waits for them, and re-layouts  13.2 us (5%)
  other arithmetic  4.95 us (2%)
    all_gather x1, blocking collectives, gather_beams(): lax.all_gather(beam_terms.reshape(1, 16, 128), 'vert', axis=0, tiled=True)  40.6 us
    all_gather x1, waiting for transfers between devices, gather_beams(): return lax.all_gather(table, 'au', axis=0, tiled=True)  31.7 us
    all_to_all x2, waiting for transfers between devices, exchange(): lax.all_to_all(value.reshape(parts, rows // parts, cols), axis, split_axi...  29.8 us
    all_to_all x1, waiting for transfers between devices, on_device(): lax.all_to_all(slots, 'vert', split_axis=0, concat_axis=0, tiled=True)  25.3 us
    all_to_all x2, starting transfers between devices, exchange(): lax.all_to_all(value.reshape(parts, rows // parts, cols), axis, split_axi...  18.9 us
    all_to_all x1, blocking collectives, exchange(): lax.all_to_all(value.reshape(parts, rows // parts, cols), axis, split_axi...  17.2 us
    pallas_call x1, Pallas kernels, sky_call(): pl.pallas_call(sky_kernel, out_shape=jax.ShapeDtypeStruct((NS, 64, 32), F...  13.3 us
    pallas_call x1, Pallas kernels, uv_call(): pl.pallas_call(uv_kernel, out_shape=(jax.ShapeDtypeStruct((512, 128), BF)...  10 us
  transfers between devices with their start and end apart: 5, of which 5 were waited for; matrix products, arithmetic and copies ran while one was open for 5% of the time, Pallas kernels for 9%

profile of v1, /device:TPU:1, one launch (start us, length us, event | category | flops | bytes accessed | tf_op | source)
XLA Modules:
  0.0 251.4 jit_solution(1546674962710456539)
XLA Ops:
  7.2 0.0 all-gather.2.cloned.1.call-start
  7.2 0.7 reshape.328
  7.9 40.6 %all_gather.6 = bf16[32,16,128]{2,1,0:T(8,128)(2,1)} all-gather(bf16[1,16,128]{2,1,0:T(8,128)(2,1)S(1)} %reshape.328), channel_id=1, replica_groups=mesh['au'=16,'vert'=32] {'vert'}, dimensions={0}, use_global_device_ids=true | all-gather | bytes 135168 | tf_op jit(solution)/shard_map/all_gather | solution.py:374
  48.5 0.0 all-gather.2.cloned.1.call-update
  48.5 1.4 copy.35.st_ref
  49.8 1.3 copy.42
  51.2 0.7 broadcast_in_dim.4
  51.9 0.7 reshape.327.scale_ref
  52.5 0.8 and_select_fusion.1
  53.3 0.6 pad.4.meta_ref
  53.9 0.7 and_select_fusion.6
  54.6 0.8 fusion.5
  55.4 0.2 convert_reduce_fusion
  55.6 0.6 stack.7.ints_ref
  56.2 1.7 convert_bitcast_fusion.vis_ref
  57.9 13.3 %sky.1.sky_ref = f32[24,64,32]{2,1,0:T(8,128)} custom-call(f32[2,24,2048]{2,1,0:T(8,128)} %convert_bitcast_fusion.vis_ref, f32[2,24,128]{2,1,0:T(8,128)} %bitcast.63, f32[1,2048]{1,0:T(1,128)} %reshape.327.scale_ref), custom_call_target="tpu_custom_call" | custom-call | flops 8053063680 | bytes 4194304 | tf_op jit(solution)/shard_map/sky/pallas_call | solution.py:111
  71.2 31.7 %all-gather.2.cloned.1.call-done.beam_ref = bf16[512,16,128]{2,1,0:T(8,128)(2,1)} async-done(((bf16[32,16,128]{2,1,0:T(8,128)(2,1)}), bf16[512,16,128]{2,1,0:T(8,128)(2,1)}) %all-gather.2.cloned.1.call-update) | async-done | bytes 2097168 | tf_op jit(solution)/shard_map/all_gather | solution.py:375
  102.9 10.0 %uv.1 = (bf16[512,128]{1,0:T(8,128)(2,1)}, bf16[32,48,128]{2,1,0:T(8,128)(2,1)}) custom-call(s32[24,2]{1,0:T(8,128)} %copy.35.st_ref, s32[7,24]{1,0:T(8,128)} %stack.7.ints_ref, f32[24]{0:T(128)} %depth_ref.1, f32[24,64,32]{2,1,0:T(8,128)} %sky.1.sky_ref, bf16[512,16,128]{2,1,0:T(8,128)(2,1)} %all-gather.2.cloned.1.call-done.beam_ref, ...), custom_call_target="tpu_custom_call" | custom-call | tf_op jit(solution)/shard_map/uv/pallas_call | solution.py:199
  112.9 14.6 %all-to-all-start.1 = ((bf16[32,16,128]{2,1,0:T(8,128)(2,1)}), bf16[32,16,128]{2,1,0:T(8,128)(2,1)S(1)}, u32[]{:S(2)}, u32[]{:S(2)}) async-start(bf16[32,16,128]{2,1,0:T(8,128)(2,1)} %bitcast.61), calls=%async_computation.1 | async-start | bytes 262144 | tf_op jit(solution)/shard_map/all_to_all | solution.py:380
  127.5 15.8 %all-to-all-done.1 = bf16[32,16,128]{2,1,0:T(8,128)(2,1)S(1)} async-done(((bf16[32,16,128]{2,1,0:T(8,128)(2,1)}), bf16[32,16,128]{2,1,0:T(8,128)(2,1)S(1)}, u32[]{:S(2)}, u32[]{:S(2)}) %all-to-all-start.1) | async-done | bytes 131104 | tf_op jit(solution)/shard_map/all_to_all | solution.py:380
  143.3 0.0 copy-start.3
  143.3 0.7 copy-done.3
  144.0 4.9 %rows.1 = bf16[768,512]{1,0:T(8,128)(2,1)} custom-call(s32[1]{0:T(128)} %bitcast.12.me_ref, bf16[512,128]{1,0:T(8,128)(2,1)} %bitcast.60, bf16[256,512]{1,0:T(8,128)(2,1)} %constant.92.clone.stage1_ref, f32[2,32,256]{2,1,0:T(8,128)} %constant.93.clone.twist_ref, bf16[64,64]{1,0:T(8,128)(2,1)} %constant.94.clone.stage2_ref), custom_call_target="tpu_custom_call" | custom-call | tf_op jit(solution)/shard_map/rows/pallas_call | solution.py:280
  148.8 17.2 %all_to_all.20 = bf16[16,48,512]{2,1,0:T(8,128)(2,1)} all-to-all(bf16[16,48,512]{2,1,0:T(8,128)(2,1)} %bitcast.57), channel_id=1, replica_groups=mesh['au'=16,'vert'=32] {'au'}, dimensions={0} | all-to-all | bytes 1572864 | tf_op jit(solution)/shard_map/all_to_all | solution.py:380
  166.0 6.4 %all-to-all-start = ((bf16[32,48,128]{2,1,0:T(8,128)(2,1)}), bf16[32,48,128]{2,1,0:T(8,128)(2,1)S(1)}, u32[]{:S(2)}, u32[]{:S(2)}) async-start(bf16[32,48,128]{2,1,0:T(8,128)(2,1)} %get-tuple-element.4), calls=%async_computation | async-start | bytes 786432 | tf_op jit(solution)/shard_map/all_to_all | solution.py:401
  172.5 2.6 %high.1 = bf16[512,512]{1,0:T(8,128)(2,1)} custom-call(s32[1]{0:T(128)} %bitcast.12.me_ref, bf16[768,512]{1,0:T(8,128)(2,1)} %bitcast.56, bf16[512,512]{1,0:T(8,128)(2,1)} %constant.95.clone.table_ref), custom_call_target="tpu_custom_call" | custom-call | tf_op jit(solution)/shard_map/high/pallas_call | solution.py:309
  175.1 25.3 %all-to-all-done.recv_ref = bf16[32,48,128]{2,1,0:T(8,128)(2,1)S(1)} async-done(((bf16[32,48,128]{2,1,0:T(8,128)(2,1)}), bf16[32,48,128]{2,1,0:T(8,128)(2,1)S(1)}, u32[]{:S(2)}, u32[]{:S(2)}) %all-to-all-start) | async-done | bytes 393248 | tf_op jit(solution)/shard_map/all_to_all | solution.py:401
  200.4 0.0 copy-start.2
  200.4 4.4 %all-to-all-start.3 = ((bf16[32,16,512]{2,1,0:T(8,128)(2,1)}), bf16[32,16,512]{2,1,0:T(8,128)(2,1)S(1)}, u32[]{:S(2)}, u32[]{:S(2)}) async-start(bf16[32,16,512]{2,1,0:T(8,128)(2,1)} %bitcast.59), calls=%async_computation.3 | async-start | bytes 1048576 | tf_op jit(solution)/shard_map/all_to_all | solution.py:380
  204.8 0.1 fusion.6
  204.9 0.7 maximum_convert_fusion.notes_ref
  205.5 0.0 copy-done.2
  205.6 7.7 %tile.1 = f32[17,2,32,256]{3,2,1,0:T(8,128)} custom-call(s32[32,6]{1,0:T(8,128)} %maximum_convert_fusion.notes_ref, bf16[32,48,128]{2,1,0:T(8,128)(2,1)} %copy-done.2, bf16[128,1024]{1,0:T(8,128)(2,1)} %constant.97.clone.rep_ref), custom_call_target="tpu_custom_call" | custom-call | tf_op jit(solution)/shard_map/tile/pallas_call | solution.py:365
  213.2 0.0 copy-start
  213.2 0.0 slice-start
  213.2 1.0 fusion.2
  214.2 2.2 collective-permute-start
  216.4 5.9 %collective-permute-done = bf16[2,32,256]{2,1,0:T(8,128)(2,1)S(1)} collective-permute-done((bf16[2,32,256]{2,1,0:T(8,128)(2,1)S(1)}, bf16[2,32,256]{2,1,0:T(8,128)(2,1)S(1)}, u32[]{:S(2)}, u32[]{:S(2)}) %collective-permute-start) | collective-permute-done | bytes 32800 | tf_op jit(solution)/shard_map/ppermute | solution.py:408
  222.3 0.0 copy-done
  222.3 0.0 slice-done
  222.3 0.1 maximum_bitcast_fusion
  222.4 0.1 copy.36
  222.5 1.8 copy.37
  224.3 14.0 %all-to-all-done.3 = bf16[32,16,512]{2,1,0:T(8,128)(2,1)S(1)} async-done(((bf16[32,16,512]{2,1,0:T(8,128)(2,1)}), bf16[32,16,512]{2,1,0:T(8,128)(2,1)S(1)}, u32[]{:S(2)}, u32[]{:S(2)}) %all-to-all-start.3) | async-done | bytes 524320 | tf_op jit(solution)/shard_map/all_to_all | solution.py:380
  238.3 0.0 copy-start.1
  238.3 0.8 copy-done.1
  239.1 2.6 %low.1 = f32[16,64,256]{2,1,0:T(8,128)} custom-call(bf16[512,512]{1,0:T(8,128)(2,1)} %bitcast.58, bf16[64,64]{1,0:T(8,128)(2,1)} %constant.96.clone.table_ref), custom_call_target="tpu_custom_call" | custom-call | tf_op jit(solution)/shard_map/low/pallas_call | solution.py:330
  241.7 2.9 %reshape.337 = f32[16,2,8192]{2,1,0:T(2,128)} reshape(f32[16,64,256]{2,1,0:T(8,128)} %low.1) | data formatting | bytes 2097152 | tf_op jit(solution)/shard_map/reshape | solution.py:404
  (4 shorter events, 0.0 us)
Async XLA Ops:
  7.2 95.7 %all-gather.2.cloned.1.call-start = ((), (), s32[]{:S(2)}) async-start(), calls=%async_computation.4 | async-start | bytes 2228224 | tf_op jit(solution)/shard_map/all_gather | solution.py:375
  112.9 30.4 %all-to-all-start.1 = ((bf16[32,16,128]{2,1,0:T(8,128)(2,1)}), bf16[32,16,128]{2,1,0:T(8,128)(2,1)S(1)}, u32[]{:S(2)}, u32[]{:S(2)}) async-start(bf16[32,16,128]{2,1,0:T(8,128)(2,1)} %bitcast.61), calls=%async_computation.1 | async-start | bytes 262144 | tf_op jit(solution)/shard_map/all_to_all | solution.py:380
  143.3 0.7 copy-start.3
  166.0 34.3 %all-to-all-start = ((bf16[32,48,128]{2,1,0:T(8,128)(2,1)}), bf16[32,48,128]{2,1,0:T(8,128)(2,1)S(1)}, u32[]{:S(2)}, u32[]{:S(2)}) async-start(bf16[32,48,128]{2,1,0:T(8,128)(2,1)} %get-tuple-element.4), calls=%async_computation | async-start | bytes 786432 | tf_op jit(solution)/shard_map/all_to_all | solution.py:401
  200.4 5.2 %copy-start.2 = (bf16[32,48,128]{2,1,0:T(8,128)(2,1)}, bf16[32,48,128]{2,1,0:T(8,128)(2,1)S(1)}, u32[]{:S(2)}) copy-start(bf16[32,48,128]{2,1,0:T(8,128)(2,1)S(1)} %all-to-all-done.recv_ref) | copy-start | bytes 1179652
  200.4 37.9 %all-to-all-start.3 = ((bf16[32,16,512]{2,1,0:T(8,128)(2,1)}), bf16[32,16,512]{2,1,0:T(8,128)(2,1)S(1)}, u32[]{:S(2)}, u32[]{:S(2)}) async-start(bf16[32,16,512]{2,1,0:T(8,128)(2,1)} %bitcast.59), calls=%async_computation.3 | async-start | bytes 1048576 | tf_op jit(solution)/shard_map/all_to_all | solution.py:380
  213.2 9.1 %copy-start = (f32[17,2,32,256]{3,2,1,0:T(8,128)S(1)}, f32[17,2,32,256]{3,2,1,0:T(8,128)}, u32[]{:S(2)}) copy-start(f32[17,2,32,256]{3,2,1,0:T(8,128)} %tile.1) | copy-start | bytes 3342340
  213.2 9.1 %slice-start = ((f32[17,2,32,256]{3,2,1,0:T(8,128)}), f32[15,2,32,256]{3,2,1,0:T(8,128)S(1)}, s32[]{:S(2)}) async-start(f32[17,2,32,256]{3,2,1,0:T(8,128)} %tile.1), calls=%async_computation.5 | async-start | bytes 1966080 | tf_op jit(solution)/shard_map/slice | solution.py:410
  214.2 8.1 %collective-permute-start = (bf16[2,32,256]{2,1,0:T(8,128)(2,1)S(1)}, bf16[2,32,256]{2,1,0:T(8,128)(2,1)S(1)}, u32[]{:S(2)}, u32[]{:S(2)}) collective-permute-start(bf16[2,32,256]{2,1,0:T(8,128)(2,1)S(1)} %fusion.2), channel_id=1, source_target_pairs={{0,32},{32,64},{64,96},{96,128},{128,160},{160,192},{192,224},{224... | collective-permute-start | bytes 98312 | tf_op jit(solution)/shard_map/ppermute | solution.py:408
  238.3 0.8 copy-start.1
Sparse Core Ops, SparseCore 0:
  48.6 54.2 all-gather.1

commit v2 on v1

v2 whole, which is shorter than its diff:
```python
import math
import numpy as np
import jax
import jax.numpy as jnp
from jax import lax
from jax.experimental import pallas as pl
from jax.experimental.pallas import tpu as pltpu

SUB = 32
NS = 24
NK = 2048
F32 = jnp.float32
BF = jnp.bfloat16
VM = pl.BlockSpec(memory_space=pltpu.VMEM)
SM = pl.BlockSpec(memory_space=pltpu.SMEM)


def cmul(ar, ai, br, bi):
    return ar * br - ai * bi, ar * bi + ai * br


def base_phase(theta):
    t = theta * theta
    s = F32(0.0)
    for n in range(17, 1, -2):
        s = (s + F32((-1.0) ** ((n - 1) // 2) / math.factorial(n))) * t
    c = F32(0.0)
    for n in range(18, 0, -2):
        c = (c + F32((-1.0) ** (n // 2) / math.factorial(n))) * t
    return c + F32(1.0), theta * (s + F32(1.0))


def dft_tables():
    x = np.arange(32) - 16
    phi = 2.0 * np.pi / 32 * (x[:, None] * x[None, :] % 32)
    c, s = np.cos(phi) / 32, np.sin(phi) / 32
    left = np.block([[c, s], [-s, c]])
    right = np.concatenate([c, s], axis=1)
    return left.astype(np.float32), right.astype(np.float32)


def phase_table(rows, cols, period):
    phi = 2.0 * np.pi / period * (np.arange(rows)[:, None] * np.arange(cols)[None, :] % period)
    return np.cos(phi), np.sin(phi)


NG = 17


def row_tables():
    c, s = phase_table(256, 256, 256)
    stage1 = np.concatenate([c, s], axis=1)
    twist = np.stack(phase_table(32, 256, 8192))
    c, s = phase_table(32, 32, 32)
    full = np.stack([np.concatenate([c, -s], axis=1), np.concatenate([s, c], axis=1)])
    stage2 = full.reshape(2, 16, 2, 64).transpose(2, 0, 1, 3).reshape(64, 64)
    return stage1, twist, stage2


def high_table():
    c, s = phase_table(256, 256, 256)
    return np.block([[c, s], [-s, c]])


def low_table():
    c, s = phase_table(32, 32, 32)
    return np.block([[c, -s], [s, c]])


def step_setup(vis_ref, off_ref, scale_ref, zu, mu, zv):
    time_id = lax.broadcasted_iota(jnp.int32, (128, NK), 0)
    k_id = lax.broadcasted_iota(jnp.int32, (128, NK), 1)
    spread = (lax.shift_right_logical(k_id, 4) == time_id).astype(F32)
    scale = scale_ref[...] * F32(2.0 * math.pi / SUB)

    def put(dest, n, pair):
        for part in range(2):
            for lo in range(0, NK, 128):
                dest[n + part, lo // 128, 0:NS, :] = pair[part][:, lo:lo + 128]

    for axis in range(2):
        shift = jnp.dot(off_ref[axis], spread, precision=lax.Precision.HIGHEST, preferred_element_type=F32)
        e1 = base_phase(shift * scale)
        e2 = cmul(*e1, *e1)
        e4 = cmul(*e2, *e2)
        e8 = cmul(*e4, *e4)
        e16 = cmul(*e8, *e8)
        dest = (zu, zv)[axis]
        put(dest, 0, e1)
        put(dest, 2, e2)
        put(dest, 4, e4)
        if axis == 1:
            put(zv, 6, e8)
            put(zv, 8, e16)
        else:
            vis = vis_ref[0], vis_ref[1]
            put(mu, 0, cmul(*vis, e16[0], -e16[1]))
            put(mu, 2, cmul(*vis, e8[0], -e8[1]))
            put(mu, 4, vis)
            put(mu, 6, cmul(*vis, *e8))


def step_sky(first, last, zu, mu, zv, wp, sky):
    row = lax.broadcasted_iota(jnp.int32, (8, 128), 0)
    bit0, bit1, bit2 = [(lax.shift_right_logical(row, n) & 1) == 1 for n in range(3)]
    one = jnp.ones((8, 128), F32)
    zero = jnp.zeros((8, 128), F32)

    def wide(ref, n, s, chunk):
        return ref[n, chunk, pl.ds(s, 8, stride=0), :]

    def base_tile(ref, s, ch):
        tr = jnp.where(bit0, wide(ref, 0, s, ch), one)
        ti = jnp.where(bit0, wide(ref, 1, s, ch), zero)
        tr, ti = cmul(tr, ti, jnp.where(bit1, wide(ref, 2, s, ch), one), jnp.where(bit1, wide(ref, 3, s, ch), zero))
        return cmul(tr, ti, jnp.where(bit2, wide(ref, 4, s, ch), one), jnp.where(bit2, wide(ref, 5, s, ch), zero))

    def one_subgrid(s, slot):
        for ch in range(NK // 128):
            lo = ch * 128
            br, bi = base_tile(zu, s, ch)
            left = [cmul(br, bi, wide(mu, 2 * n, s, ch), wide(mu, 2 * n + 1, s, ch)) for n in range(4)]
            br, bi = base_tile(zv, s, ch)
            e8r, e8i = wide(zv, 6, s, ch), wide(zv, 7, s, ch)
            e16r, e16i = wide(zv, 8, s, ch), wide(zv, 9, s, ch)
            right = [cmul(br, bi, e16r, -e16i), cmul(br, bi, e8r, -e8i), (br, bi), cmul(br, bi, e8r, e8i)]
            for side, blocks in enumerate((left, right)):
                for part in range(2):
                    for half in range(2):
                        at = side * 64 + part * 32 + half * 16
                        wp[slot, at:at + 16, lo:lo + 128] = jnp.concatenate(
                            [blocks[2 * half][part], blocks[2 * half + 1][part]], axis=0).astype(BF)

    def finish(s, slot):
        prod = lax.dot_general(wp[slot, 0:64, :], wp[slot, 64:128, :], (((1,), (1,)), ((), ())), preferred_element_type=F32)
        sky[s, 0:32, :] = prod[0:32, 0:32] - prod[32:64, 32:64]
        sky[s, 32:64, :] = prod[0:32, 32:64] + prod[32:64, 0:32]

    def pair(i, _):
        one_subgrid(2 * i, 0)
        one_subgrid(2 * i + 1, 1)
        finish(2 * i, 0)
        finish(2 * i + 1, 1)
        return 0

    lax.fori_loop(first, last, pair, 0)


def pixel_ids():
    x = lax.broadcasted_iota(jnp.int32, (8, 128), 0)
    lane = lax.broadcasted_iota(jnp.int32, (8, 128), 1)
    return 4 * x + lax.shift_right_logical(lane, 5) - 16, (lane & 31) - 16


def unfold(re, im, box):
    for y in range(4):
        ra = re if y == 0 else pltpu.roll(re, 128 - 32 * y, 1)
        rb = im if y == 0 else pltpu.roll(im, 128 - 32 * y, 1)
        box[pl.ds(y, 8, stride=4), :] = ra
        box[pl.ds(32 + y, 8, stride=4), :] = rb
    return box[0:32, 0:32], box[32:64, 0:32]


def step_screen(ints_ref, depth_ref, sky, box):
    p, q = pixel_ids()
    pf, qf = p.astype(F32), q.astype(F32)
    ap, aq = pf * F32(0.1 / 32), qf * F32(0.1 / 32)
    rad = ap * ap + aq * aq
    tp = (2.0 * pf + 1.0) * F32(1.0 / 32)
    tq = (2.0 * qf + 1.0) * F32(1.0 / 32)
    taper = (1.0 - tp * tp) * (1.0 - tq * tq) * F32(1.0 / math.sqrt(NK))

    def one(s, _):
        turn = (ints_ref[0, s] * p + ints_ref[1, s] * q) & 31
        ang = turn.astype(F32) * F32(2.0 * math.pi / 32) - F32(math.pi) * depth_ref[s] * rad
        kr, ki = unfold(jnp.cos(ang) * taper, jnp.sin(ang) * taper, box)
        cr, ci = cmul(sky[s, 0:32, :], sky[s, 32:64, :], kr, ki)
        sky[s, 0:32, :] = cr
        sky[s, 32:64, :] = ci
        return 0

    lax.fori_loop(0, NS, one, 0)


def step_uv(ints_ref, sky, table, meta_ref, left_ref, right_ref, box, g_ref, rb):
    def one(s, _):
        a = table[ints_ref[2, s]].astype(F32)
        b = table[ints_ref[3, s]].astype(F32)
        pr = a[0:8] * b[0:8] + a[8:16] * b[8:16]
        pi_ = a[8:16] * b[0:8] - a[0:8] * b[8:16]
        kr, ki = unfold(pr, pi_, box)
        cr, ci = cmul(sky[s, 0:32, :], sky[s, 32:64, :], kr, ki)
        cor = jnp.concatenate([cr, ci], axis=0).astype(BF)
        g = jnp.dot(left_ref[...], cor, preferred_element_type=F32)
        g_ref[pl.ds(pl.multiple_of(s * 64, 64), 64), :] = g.astype(BF)
        return 0

    lax.fori_loop(0, NS, one, 0)

    def two(y, _):
        outs = []
        for half in range(2):
            s = y + 12 * half
            yv = jnp.dot(g_ref[pl.ds(pl.multiple_of(s * 64, 64), 64), :], right_ref[...], preferred_element_type=F32)
            outs.append(yv[0:32, 0:32] + yv[32:64, 32:64])
            outs.append(yv[32:64, 0:32] - yv[0:32, 32:64])
        rb[pl.ds(y, 32, stride=16), :] = jnp.concatenate(outs, axis=1)
        return 0

    lax.fori_loop(0, 12, two, 0)
    for n in range(4):
        rb[pl.ds(12 + n, 32, stride=16), :] = jnp.broadcast_to(meta_ref[n:n + 1, :], (32, 128))


def step_slots(rb, place_ref, scr, slot_send):
    low = lax.broadcasted_iota(jnp.int32, (32, 128), 1) < 64

    def one(c, _):
        x = rb[pl.ds(pl.multiple_of(c * 16, 16), 16), :]
        both = jnp.concatenate([x, pltpu.roll(x, 64, 1)], axis=0).astype(BF)
        z = jnp.dot(place_ref[...], both, preferred_element_type=F32)
        scr[pl.ds(c, 32, stride=32), :] = jnp.where(low, z[0:32], z[32:64])
        return 0

    lax.fori_loop(0, 32, one, 0)
    slot_send[...] = scr[...].reshape(32, 32, 128).astype(BF)


def step_rows(me, rows_recv, stage1_ref, twist_ref, stage2_ref, scr, lhs, oht, yv, buf, sbuf, high_send, spill_send):
    scr[...] = rows_recv[...].reshape(512, 128).astype(F32)
    lane = lax.broadcasted_iota(jnp.int32, (32, 768), 1)
    src = lax.broadcasted_iota(jnp.int32, (32, 768), 0)
    pick_src = ((lane & 31) == src).astype(BF)
    pick_item = lax.shift_right_logical(lane, 5) == src

    def meta(n):
        table = jnp.transpose(scr[pl.ds(12 + n, 32, stride=16), :])[0:32]
        spread = jnp.dot(table.astype(BF), pick_src, preferred_element_type=F32)
        return jnp.sum(jnp.where(pick_item, spread, 0.0), axis=0, keepdims=True)

    g_hi, g_lo, h, e = [meta(n) for n in range(4)]
    g = g_hi + jnp.where(g_lo > me.astype(F32), 1.0, 0.0)
    h_id = lax.broadcasted_iota(jnp.int32, (256, 768), 0).astype(F32)
    oht[:, 0:768] = (h_id == h).astype(BF)
    oht[:, 768:1536] = (h_id == h + 1.0).astype(BF)
    col = (lax.broadcasted_iota(jnp.int32, (64, 384), 0) & 31).astype(F32)
    for half in range(2):
        parts = []
        for blk in range(3):
            rows = jnp.concatenate([scr[pl.ds(4 * blk + n, 32, stride=16), :] for n in range(4)], axis=0)
            parts.append(jnp.transpose(rows)[half * 64:half * 64 + 64])
        v = jnp.concatenate(parts, axis=1)
        at = half * 384
        first = col >= e[:, at:at + 384]
        hi = jnp.where(first, v, 0.0)
        lo = jnp.where(first, 0.0, v)
        for n in range(NG):
            here = g[:, at:at + 384] == float(n)
            lhs[n * 64:n * 64 + 64, at:at + 384] = jnp.where(here, hi, 0.0).astype(BF)
            lhs[n * 64:n * 64 + 64, 768 + at:768 + at + 384] = jnp.where(here, lo, 0.0).astype(BF)
    x = lax.dot_general(lhs[...], oht[...], (((1,), (1,)), ((), ())), preferred_element_type=F32).astype(BF)
    yv[...] = jnp.dot(x, stage1_ref[...], preferred_element_type=F32)
    for n in range(NG):
        y = yv[n * 64:n * 64 + 64, :]
        re = y[0:32, 0:256] - y[32:64, 256:512]
        im = y[0:32, 256:512] + y[32:64, 0:256]
        re, im = cmul(re, im, twist_ref[0], twist_ref[1])
        z = jnp.dot(stage2_ref[...], jnp.concatenate([re, im], axis=0).astype(BF), preferred_element_type=F32)
        for low in range(2):
            for comp in range(2):
                for k in range(2):
                    at = (low * 2 + comp) * 16
                    piece = z[at:at + 16, k * 128:k * 128 + 128]
                    if n < 16:
                        buf[low * 2 + k, pl.ds(comp * 16 + n, 16, stride=32), :] = piece
                    else:
                        sbuf[pl.ds(comp * 4 + low * 2 + k, 16, stride=16), :] = piece
    for k in range(4):
        high_send[:, :, k * 128:k * 128 + 128] = buf[k].reshape(16, 32, 128).astype(BF)
    spill_send[...] = sbuf[...].reshape(16, 16, 128).astype(BF)


def step_high(me, high_recv, spill_recv, table_ref, xh, low_send):
    first = lax.broadcasted_iota(jnp.int32, (16, 512), 0) == 0
    for r in range(16):
        spill = spill_recv[(r + 15) % 16].astype(F32)
        for comp in range(2):
            block = high_recv[r, comp * 16:comp * 16 + 16, :].astype(F32)
            line = jnp.concatenate([spill[comp * 4 + k:comp * 4 + k + 1] for k in range(4)], axis=1)
            xh[comp * 256 + r * 16:comp * 256 + r * 16 + 16, :] = jnp.where(first, block + line, block).astype(BF)
    y = lax.dot_general(xh[...], table_ref[...], (((0,), (0,)), ((), ())), preferred_element_type=F32)
    ql = lax.broadcasted_iota(jnp.int32, (8, 256), 1)
    ang = (ql * me).astype(F32) * F32(2.0 * math.pi / 8192)
    re, im = cmul(y[:, 0:256], y[:, 256:512], jnp.cos(ang)[0:1], jnp.sin(ang)[0:1])
    low_send[:, :, 0:256] = re.reshape(32, 16, 256).astype(BF)
    low_send[:, :, 256:512] = im.reshape(32, 16, 256).astype(BF)


def step_low(low_recv, table_ref, scr, out_ref):
    for k in range(4):
        scr[k] = low_recv[:, :, k * 128:k * 128 + 128].reshape(512, 128).astype(F32)
    for m in range(16):
        parts = [jnp.concatenate([scr[2 * comp + k, pl.ds(m, 32, stride=16), :] for k in range(2)], axis=1) for comp in range(2)]
        x = jnp.concatenate(parts, axis=0).astype(BF)
        out_ref[m] = jnp.dot(table_ref[...], x, preferred_element_type=F32) * F32(1.0 / (SUB * math.sqrt(12288)))


def step_tile(me, scr, slot_recv, vals, spare, tile_ref, tail_send):
    vals[...] = slot_recv[...].reshape(1024, 128).astype(F32)
    hi, lo, h, e = [scr[pl.ds(12 + n, 32, stride=16), :] for n in range(4)]
    lane = lax.broadcasted_iota(jnp.int32, (32, 128), 1)
    base = me.astype(F32) * 8.0
    mine = (h >= base) & (h < base + 8.0) & (lane < NS)
    upto = (lax.broadcasted_iota(jnp.int32, (128, 128), 0) < lax.broadcasted_iota(jnp.int32, (128, 128), 1)).astype(BF)
    order = jnp.dot(mine.astype(BF), upto, preferred_element_type=F32)
    start = (h - base) * 32.0 + e
    column = lax.broadcasted_iota(jnp.int32, (32, 256), 1).astype(F32)
    seen, his, los = [], [], []
    for rank in range(2):
        pick = mine & (order == float(rank))
        hit = jnp.sum(jnp.where(pick, 1.0, 0.0), axis=1, keepdims=True)
        low_edge = jnp.sum(jnp.where(pick, start, 0.0), axis=1, keepdims=True)
        seen.append((column >= low_edge) & (column < low_edge + 32.0 * hit))
        for box, values in ((his, hi), (los, lo)):
            one = jnp.sum(jnp.where(pick, values, 0.0), axis=1, keepdims=True)
            box.append(jnp.transpose(jnp.broadcast_to(one, (32, 128)))[0:1, :])
    hi_line = jnp.concatenate(his, axis=1)
    lo_line = jnp.concatenate(los, axis=1)
    g_id = lax.broadcasted_iota(jnp.int32, (32, 64), 0).astype(F32)
    quarter = lax.shift_right_logical(lane, 5)

    def one(c, _):
        x = vals[pl.ds(c, 32, stride=32), :]
        lines = []
        for rank in range(2):
            for comp in range(2):
                y = jnp.where(quarter == rank * 2 + comp, x, 0.0)
                y = y + pltpu.roll(y, 32, 1)
                y = y + pltpu.roll(y, 64, 1)
                lines.append(jnp.where(seen[rank], jnp.concatenate([y, y], axis=1), 0.0))
        rhs = jnp.concatenate([jnp.concatenate(lines[0:2], axis=1), jnp.concatenate(lines[2:4], axis=1)], axis=0).astype(BF)
        where = hi_line + jnp.where(lo_line > c.astype(F32), 1.0, 0.0)
        z = jnp.dot((g_id == where).astype(BF), rhs, preferred_element_type=F32)
        for k in range(4):
            tile_ref[k, pl.ds(c, 16, stride=32), :] = z[0:16, k * 128:k * 128 + 128]
            spare[k, pl.ds(pl.multiple_of(c * 8, 8), 8), :] = z[16:24, k * 128:k * 128 + 128]
        return 0

    lax.fori_loop(0, 32, one, 0)
    for k in range(4):
        tail_send[k] = spare[k, pl.ds(0, 32, stride=8), :].astype(BF)


MESH = pl.DeviceIdType.MESH


def whole_kernel(ints_ref, depth_ref, vis_ref, off_ref, scale_ref, beam_ref, meta_ref, place_ref,
                 left_ref, right_ref, stage1_ref, twist_ref, stage2_ref, high_ref, low_ref,
                 dirty_ref, tile_ref,
                 table, zu, mu, zv, wp, sky, box, g_ref, rb, rows_send, rows_recv, scr, lhs, oht, yv, buf, sbuf,
                 high_send, high_recv, spill_send, spill_recv, xh, low_send, low_recv, slot_scr, slot_send, slot_recv,
                 spare, tail_send, tail_recv, sem1, sem2, sem3, sem4, sem5, sem6, sem7, sem8, sem9, local_sem):
    au, me = lax.axis_index("au"), lax.axis_index("vert")
    z, core = me // 2, me % 2
    NZ, NA, NV = 16, 16, 32

    def remote(src, dst, sems, k, to):
        return pltpu.make_async_remote_copy(src_ref=src, dst_ref=dst, send_sem=sems.at[0, k], recv_sem=sems.at[1, k],
                                            device_id=to, device_id_type=MESH)

    def loop(first, last, body):
        lax.fori_loop(first, last, lambda k, _: (body(k), 0)[1], 0)

    barrier = pltpu.get_barrier_semaphore()
    loop(1, NV, lambda k: pl.semaphore_signal(barrier, inc=1, device_id=(au, (me + k) % NV), device_id_type=MESH))
    loop(1, NA, lambda k: pl.semaphore_signal(barrier, inc=1, device_id=((au + k) % NA, me), device_id_type=MESH))

    def spot(core, au, z):
        return (core * NA + au) * NZ + z

    def along_z(k, back):
        peer = (z + NZ - k) % NZ if back else (z + k) % NZ
        return remote(beam_ref.at[0], table.at[spot(core, au, peer if back else z)], sem1, k, (au, peer * 2 + core))

    def over_au(k, back):
        peer = (au + NA - k) % NA if back else (au + k) % NA
        at = table.at[pl.ds(spot(core, peer if back else au, 0), NZ)]
        return remote(at, at, sem2, k, (peer, me))

    def partner(k, back):
        at = table.at[pl.ds(spot(1 - core if back else core, (au + NA - k) % NA, 0), NZ)]
        return remote(at, at, sem3, k, (au, z * 2 + 1 - core))

    own = pltpu.make_async_copy(beam_ref.at[0], table.at[spot(core, au, z)], local_sem.at[0])
    own.start()
    step_setup(vis_ref, off_ref, scale_ref, zu, mu, zv)
    step_sky(0, 3, zu, mu, zv, wp, sky)
    pl.semaphore_wait(barrier, NV - 1 + NA - 1)
    loop(1, NZ, lambda k: along_z(k, False).start())
    step_sky(3, 10, zu, mu, zv, wp, sky)
    own.wait()
    loop(1, NZ, lambda k: along_z(k, True).wait_recv())
    loop(1, NA, lambda k: over_au(k, False).start())
    partner(0, False).start()
    step_sky(10, 12, zu, mu, zv, wp, sky)
    step_screen(ints_ref, depth_ref, sky, box)

    def relay(k):
        over_au(k, True).wait_recv()
        partner(k, False).start()

    loop(1, NA, relay)
    loop(0, NA, lambda k: partner(k, True).wait_recv())
    step_uv(ints_ref, sky, table, meta_ref, left_ref, right_ref, box, g_ref, rb)
    rows_send[...] = rb[...].reshape(32, 16, 128).astype(BF)

    def along_vert(send, recv, sems, k, back):
        peer = (me + NV - k) % NV if back else (me + k) % NV
        return remote(send.at[peer], recv.at[peer if back else me], sems, k, (au, peer))

    def across_au(send, recv, sems, k, back):
        peer = (au + NA - k) % NA if back else (au + k) % NA
        return remote(send.at[peer], recv.at[peer if back else au], sems, k, (peer, me))

    loop(1, NV, lambda k: along_vert(rows_send, rows_recv, sem4, k, False).start())
    rows_recv[me] = rows_send[me]
    step_slots(rb, place_ref, slot_scr, slot_send)
    loop(1, NV, lambda k: along_vert(slot_send, slot_recv, sem5, k, False).start())
    slot_recv[me] = slot_send[me]
    loop(1, NV, lambda k: along_vert(rows_send, rows_recv, sem4, k, True).wait_recv())
    step_rows(me, rows_recv, stage1_ref, twist_ref, stage2_ref, scr, lhs, oht, yv, buf, sbuf, high_send, spill_send)
    loop(1, NA, lambda k: across_au(high_send, high_recv, sem6, k, False).start())
    loop(1, NA, lambda k: across_au(spill_send, spill_recv, sem7, k, False).start())
    high_recv[au] = high_send[au]
    spill_recv[au] = spill_send[au]
    loop(1, NA, lambda k: across_au(high_send, high_recv, sem6, k, True).wait_recv())
    loop(1, NA, lambda k: across_au(spill_send, spill_recv, sem7, k, True).wait_recv())
    step_high(me, high_recv, spill_recv, high_ref, xh, low_send)
    loop(1, NV, lambda k: along_vert(low_send, low_recv, sem8, k, False).start())
    low_recv[me] = low_send[me]
    loop(1, NV, lambda k: along_vert(slot_send, slot_recv, sem5, k, True).wait_recv())
    step_tile(me, scr, slot_recv, slot_scr, spare, tile_ref, tail_send)
    tail = remote(tail_send, tail_recv, sem9, 0, ((au + 1) % NA, me))
    tail.start()
    tail.wait_recv()
    for k in range(4):
        tile_ref[k, 0:32, :] += tail_recv[k].astype(F32)
    loop(1, NV, lambda k: along_vert(low_send, low_recv, sem8, k, True).wait_recv())
    step_low(low_recv, low_ref, buf, dirty_ref)

    loop(1, NZ, lambda k: along_z(k, False).wait_send())
    loop(1, NA, lambda k: over_au(k, False).wait_send())
    loop(0, NA, lambda k: partner(k, False).wait_send())
    loop(1, NV, lambda k: along_vert(rows_send, rows_recv, sem4, k, False).wait_send())
    loop(1, NV, lambda k: along_vert(slot_send, slot_recv, sem5, k, False).wait_send())
    loop(1, NA, lambda k: across_au(high_send, high_recv, sem6, k, False).wait_send())
    loop(1, NA, lambda k: across_au(spill_send, spill_recv, sem7, k, False).wait_send())
    loop(1, NV, lambda k: along_vert(low_send, low_recv, sem8, k, False).wait_send())
    tail.wait_send()


def whole_call(ints, depth, vis, off, scale, beam, meta, place):
    left, right = dft_tables()
    stage1, twist, stage2 = row_tables()
    consts = [jnp.asarray(left, BF), jnp.asarray(right, BF), jnp.asarray(stage1, BF), jnp.asarray(twist, F32),
              jnp.asarray(stage2, BF), jnp.asarray(high_table(), BF), jnp.asarray(low_table(), BF)]
    V, D = pltpu.VMEM, pltpu.SemaphoreType.DMA
    scratch = [
        V((512, 16, 128), BF), V((6, 16, 32, 128), F32), V((8, 16, 32, 128), F32), V((10, 16, 32, 128), F32), V((2, 128, NK), BF),
        V((NS, 64, 32), F32), V((64, 128), F32), V((NS * 64, 32), BF), V((512, 128), F32), V((32, 16, 128), BF), V((32, 16, 128), BF),
        V((512, 128), F32), V((NG * 64, 1536), BF), V((256, 1536), BF), V((NG * 64, 512), F32), V((4, 512, 128), F32), V((256, 128), F32),
        V((16, 32, 512), BF), V((16, 32, 512), BF), V((16, 16, 128), BF), V((16, 16, 128), BF), V((512, 512), BF),
        V((32, 16, 512), BF), V((32, 16, 512), BF), V((1024, 128), F32), V((32, 32, 128), BF), V((32, 32, 128), BF),
        V((4, 256, 128), F32), V((4, 32, 128), BF), V((4, 32, 128), BF),
        D((2, 16)), D((2, 16)), D((2, 16)), D((2, 32)), D((2, 32)), D((2, 16)), D((2, 16)), D((2, 32)), D((2, 1)), D((1,)),
    ]
    return pl.pallas_call(
        whole_kernel,
        out_shape=(jax.ShapeDtypeStruct((16, 64, 256), F32), jax.ShapeDtypeStruct((4, 512, 128), F32)),
        in_specs=[SM] * 2 + [VM] * 13, out_specs=(VM, VM),
        scratch_shapes=scratch,
        compiler_params=pltpu.CompilerParams(collective_id=0, has_side_effects=True, vmem_limit_bytes=60 << 20),
        name="whole",
    )(ints, depth, vis, off, scale, beam, meta, place, *consts)


def on_device(visibilities, baseline_offsets, channel_scale, screen_depth, stations, corners, beam_terms):
    au = lax.axis_index("au")
    row, col = corners[:, 0], corners[:, 1]
    dest = col // 256
    order = jnp.arange(NS, dtype=jnp.int32)
    rank = jnp.sum(((dest[None, :] == dest[:, None]) & (order[None, :] < order[:, None])).astype(jnp.int32), axis=1)
    spots = ((stations & 1) * 16 + stations // 32) * 16 + (stations // 2) % 16
    ints = jnp.stack([row, col, spots[:, 0], spots[:, 1]])
    meta = jnp.pad(jnp.stack([(row - au * 512) // 32, row % 32, col // 32, col % 32]).astype(F32), ((0, 0), (0, 128 - NS)))
    slot = dest + 32 * rank
    gap = jnp.full((4,), -1, jnp.int32)
    slot = jnp.stack([jnp.concatenate([slot[:12], gap, slot[12:], gap]), jnp.concatenate([slot[12:], gap, slot[:12], gap])])
    ids = jnp.arange(64, dtype=jnp.int32)
    place = (jnp.where(ids[:, None] < 32, slot[0][None, :], slot[1][None, :]) == ids[:, None]).astype(BF)
    dirty, tile = whole_call(
        ints, screen_depth,
        visibilities.transpose(1, 0, 2).astype(F32),
        baseline_offsets.transpose(1, 0, 2),
        jnp.broadcast_to(channel_scale[None, :], (128, 16)).reshape(1, NK),
        beam_terms.reshape(1, 16, 128), meta, place,
    )
    gridded = tile.reshape(2, 2, 512, 128).transpose(2, 0, 1, 3).reshape(512, 2, 256)
    return gridded, dirty.reshape(16, 2, 8192)


def solution(mesh):
    from jax.sharding import PartitionSpec as P

    both = ("au", "vert")
    return jax.shard_map(
        on_device,
        mesh=mesh,
        in_specs=(P(both, None, None), P(both, None, None), P(), P(both), P(both, None), P(both, None), P(both, None, None)),
        out_specs=(P("au", None, "vert"), P(both, None, None)),
        check_vma=False,
    )
```

time: 252 us -> 129 us (0.51)
  waiting for transfers between devices: 92.7 us -> 0 us
  Pallas kernels: 41 us -> 111 us
  blocking collectives: 57.8 us -> 0 us
  starting transfers between devices: 27.6 us -> 0 us
  between operations: 14.1 us -> 0.69 us
  local copies, waits for them, and re-layouts: 13.2 us -> 10.5 us
    pallas_call x6 -> x1, Pallas kernels: 41 us -> 111 us  [whole_call(): pl.pallas_call(whole_kernel, out_shape=(jax.ShapeDtypeStruct((16, 64, 256...]
    all_to_all x3 -> x0, waiting for transfers between devices: 55.1 us -> none  [the longest x2 29.8 us: exchange(): lax.all_to_all(value.reshape(parts, rows // parts, cols), axis, split_axi...]
    all_gather x1 -> x0, blocking collectives: 40.6 us -> none  [gather_beams(): lax.all_gather(beam_terms.reshape(1, 16, 128), 'vert', axis=0, tiled=True)]
    all_gather x1 -> x0, waiting for transfers between devices: 31.7 us -> none  [gather_beams(): return lax.all_gather(table, 'au', axis=0, tiled=True)]
    all_to_all x3 -> x0, starting transfers between devices: 25.4 us -> none  [the longest x2 18.9 us: exchange(): lax.all_to_all(value.reshape(parts, rows // parts, cols), axis, split_axi...]
    all_to_all x1 -> x0, blocking collectives: 17.2 us -> none  [exchange(): lax.all_to_all(value.reshape(parts, rows // parts, cols), axis, split_axi...]
    ppermute x1 -> x0, waiting for transfers between devices: 5.92 us -> none  [on_device(): lax.ppermute(tile[16].astype(BF), 'au', [(n, (n + 1) % 16) for n in range...]
    unnamed x12 -> x5, local copies, waits for them, and re-layouts: 5.94 us -> 1.35 us
  transfers between devices with their start and end apart: 5 -> 0, of which waited for: 5 -> 0; matrix products, arithmetic and copies ran while one was open for 5% -> 0% of each run, Pallas kernels for 9% -> 0%
where the time goes in v2:
time: 129 us; the launch traced here: 128 us
  Pallas kernels  111 us (86%)
  local copies, waits for them, and re-layouts  10.5 us (8%)
  other arithmetic  6.01 us (5%)
    pallas_call x1, Pallas kernels, whole_call(): pl.pallas_call(whole_kernel, out_shape=(jax.ShapeDtypeStruct((16, 64, 256...  111 us

profile of v2, /device:TPU:1, one launch (start us, length us, event | category | flops | bytes accessed | tf_op | source)
XLA Modules:
  0.0 128.4 jit_solution(4552091964256516333)
XLA Ops:
  0.6 0.0 copy-start.1
  0.6 0.7 and_select_fusion.1
  1.4 0.7 fusion.2
  2.1 0.8 and_select_fusion.5
  2.9 0.6 pad.4.meta_ref
  3.5 0.8 fusion.7
  4.3 0.2 convert_reduce_fusion
  4.4 0.7 multiply_add_fusion
  5.1 0.1 fusion.8
  5.2 0.1 pad_add_fusion.2
  5.3 0.6 pad_add_fusion.ints_ref
  5.9 1.3 %reshape.256.beam_ref = bf16[1,16,128]{2,1,0:T(8,128)(2,1)} reshape(bf16[1,2,1024]{2,1,0:T(2,128)(2,1)} %param.20) | data formatting | bytes 8192 | tf_op jit(solution)/shard_map/reshape | solution.py:506
  7.2 0.7 fusion.place_ref
  7.8 1.3 %copy.27 = f32[24,2,128]{2,0,1:T(8,128)} copy(f32[24,2,128]{2,1,0:T(2,128)} %param.15) | data formatting | bytes 49152 | tf_op args[1]
  9.2 0.7 broadcast_in_dim.26
  9.8 0.7 reshape.255.scale_ref
  10.5 0.0 copy-done.1
  10.5 0.8 convert_bitcast_fusion.vis_ref
  11.3 111.1 %whole.1 = (f32[16,64,256]{2,1,0:T(8,128)}, f32[4,512,128]{2,1,0:T(8,128)}) custom-call(s32[4,24]{1,0:T(4,128)} %pad_add_fusion.ints_ref, f32[24]{0:T(128)} %depth_ref.1, f32[2,24,2048]{2,1,0:T(8,128)} %convert_bitcast_fusion.vis_ref, f32[2,24,128]{2,1,0:T(8,128)} %bitcast.38, f32[1,2048]{1,0:T(1,128)} %reshape.255.scale_ref, ...), custom_call_target="tpu_custom_call" | custom-call | tf_op jit(solution)/shard_map/whole/pallas_call | solution.py:477
  122.5 2.0 %copy.24 = f32[512,2,2,128]{3,2,1,0:T(2,128)S(1)} copy(f32[512,2,2,128]{3,0,2,1:T(8,128)} %bitcast.37) | data formatting | bytes 2097152 | tf_op jit(solution)/shard_map/transpose | solution.py:508
  124.5 0.0 copy-start
  124.5 2.2 %reshape.258 = f32[512,2,256]{2,1,0:T(2,128)} reshape(f32[512,2,2,128]{3,2,1,0:T(2,128)S(1)} %copy.24) | data formatting | bytes 2097152 | tf_op jit(solution)/shard_map/reshape | solution.py:508
  126.7 0.0 copy-done
  126.7 1.7 %reshape.259 = f32[16,2,8192]{2,1,0:T(2,128)} reshape(f32[16,64,256]{2,1,0:T(8,128)S(1)} %copy-done) | data formatting | bytes 2097152 | tf_op jit(solution)/shard_map/reshape | solution.py:509
  (5 shorter events, 0.0 us)
Async XLA Ops:
  0.6 9.9 %copy-start.1 = (bf16[24,2,2048]{2,1,0:T(2,128)(2,1)S(1)}, bf16[24,2,2048]{2,1,0:T(2,128)(2,1)}, u32[]{:S(2)}) copy-start(bf16[24,2,2048]{2,1,0:T(2,128)(2,1)} %param.14) | copy-start | bytes 589828
  124.5 2.2 %copy-start = (f32[16,64,256]{2,1,0:T(8,128)S(1)}, f32[16,64,256]{2,1,0:T(8,128)}, u32[]{:S(2)}) copy-start(f32[16,64,256]{2,1,0:T(8,128)} %get-tuple-element.5) | copy-start | bytes 3145732

commit v3 on v2

v3 whole, which is shorter than its diff:
```python
import math
import numpy as np
import jax
import jax.numpy as jnp
from jax import lax
from jax.experimental import pallas as pl
from jax.experimental.pallas import tpu as pltpu

SUB = 32
NS = 24
NK = 2048
F32 = jnp.float32
BF = jnp.bfloat16
VM = pl.BlockSpec(memory_space=pltpu.VMEM)
SM = pl.BlockSpec(memory_space=pltpu.SMEM)


def cmul(ar, ai, br, bi):
    return ar * br - ai * bi, ar * bi + ai * br


def base_phase(theta):
    t = theta * theta
    s = F32(0.0)
    for n in range(17, 1, -2):
        s = (s + F32((-1.0) ** ((n - 1) // 2) / math.factorial(n))) * t
    c = F32(0.0)
    for n in range(18, 0, -2):
        c = (c + F32((-1.0) ** (n // 2) / math.factorial(n))) * t
    return c + F32(1.0), theta * (s + F32(1.0))


def dft_tables():
    x = np.arange(32) - 16
    phi = 2.0 * np.pi / 32 * (x[:, None] * x[None, :] % 32)
    c, s = np.cos(phi) / 32, np.sin(phi) / 32
    left = np.block([[c, s], [-s, c]])
    right = np.concatenate([c, s], axis=1)
    return left.astype(np.float32), right.astype(np.float32)


def phase_table(rows, cols, period):
    phi = 2.0 * np.pi / period * (np.arange(rows)[:, None] * np.arange(cols)[None, :] % period)
    return np.cos(phi), np.sin(phi)


NG = 17


def row_tables():
    c, s = phase_table(256, 256, 256)
    stage1 = np.concatenate([c, s], axis=1)
    twist = np.stack(phase_table(32, 256, 8192))
    c, s = phase_table(32, 32, 32)
    full = np.stack([np.concatenate([c, -s], axis=1), np.concatenate([s, c], axis=1)])
    stage2 = full.reshape(2, 16, 2, 64).transpose(2, 0, 1, 3).reshape(64, 64)
    return stage1, twist, stage2


def high_table():
    c, s = phase_table(256, 256, 256)
    return np.block([[c, s], [-s, c]])


def low_table():
    c, s = phase_table(32, 32, 32)
    return np.block([[c, -s], [s, c]])


def step_setup(vis_ref, off_ref, scale_ref, vs, zu, mu, zv):
    time_id = lax.broadcasted_iota(jnp.int32, (128, NK), 0)
    k_id = lax.broadcasted_iota(jnp.int32, (128, NK), 1)
    spread = (lax.shift_right_logical(k_id, 4) == time_id).astype(F32)
    channel = lax.broadcasted_iota(jnp.int32, (1, NK), 1) & 15
    scale = jnp.zeros((1, NK), F32)
    for c in range(16):
        scale = jnp.where(channel == c, scale_ref[c], scale)
    scale = scale * F32(2.0 * math.pi / SUB)
    vs[...] = vis_ref[...].astype(F32)
    chunks = range(NK // 128)

    def put(dest, n, pair):
        for part in range(2):
            for ch in chunks:
                dest[n + part, ch, 0:NS, :] = pair[part][:, ch * 128:ch * 128 + 128]

    for axis in range(2):
        shift = jnp.dot(off_ref[pl.ds(axis, NS, stride=2), :], spread, precision=lax.Precision.HIGHEST, preferred_element_type=F32)
        e1 = base_phase(shift * scale)
        e2 = cmul(*e1, *e1)
        e4 = cmul(*e2, *e2)
        e8 = cmul(*e4, *e4)
        e16 = cmul(*e8, *e8)
        dest = (zu, zv)[axis]
        put(dest, 0, e1)
        put(dest, 2, e2)
        put(dest, 4, e4)
        if axis == 1:
            put(zv, 6, e8)
            put(zv, 8, e16)
        else:
            for ch in chunks:
                vis = [vs[pl.ds(ch * 2 + part, NS, stride=32), :] for part in range(2)]
                a8 = [x[:, ch * 128:ch * 128 + 128] for x in e8]
                a16 = [x[:, ch * 128:ch * 128 + 128] for x in e16]
                for n, pair in enumerate((cmul(*vis, a16[0], -a16[1]), cmul(*vis, a8[0], -a8[1]), vis, cmul(*vis, *a8))):
                    for part in range(2):
                        mu[2 * n + part, ch, 0:NS, :] = pair[part]


def step_sky(first, last, zu, mu, zv, wp, sky):
    row = lax.broadcasted_iota(jnp.int32, (8, 128), 0)
    bit0, bit1, bit2 = [(lax.shift_right_logical(row, n) & 1) == 1 for n in range(3)]
    one = jnp.ones((8, 128), F32)
    zero = jnp.zeros((8, 128), F32)

    def wide(ref, n, s, chunk):
        return ref[n, chunk, pl.ds(s, 8, stride=0), :]

    def base_tile(ref, s, ch):
        tr = jnp.where(bit0, wide(ref, 0, s, ch), one)
        ti = jnp.where(bit0, wide(ref, 1, s, ch), zero)
        tr, ti = cmul(tr, ti, jnp.where(bit1, wide(ref, 2, s, ch), one), jnp.where(bit1, wide(ref, 3, s, ch), zero))
        return cmul(tr, ti, jnp.where(bit2, wide(ref, 4, s, ch), one), jnp.where(bit2, wide(ref, 5, s, ch), zero))

    def one_subgrid(s, slot):
        for ch in range(NK // 128):
            lo = ch * 128
            br, bi = base_tile(zu, s, ch)
            left = [cmul(br, bi, wide(mu, 2 * n, s, ch), wide(mu, 2 * n + 1, s, ch)) for n in range(4)]
            br, bi = base_tile(zv, s, ch)
            e8r, e8i = wide(zv, 6, s, ch), wide(zv, 7, s, ch)
            e16r, e16i = wide(zv, 8, s, ch), wide(zv, 9, s, ch)
            right = [cmul(br, bi, e16r, -e16i), cmul(br, bi, e8r, -e8i), (br, bi), cmul(br, bi, e8r, e8i)]
            for side, blocks in enumerate((left, right)):
                for part in range(2):
                    for half in range(2):
                        at = side * 64 + part * 32 + half * 16
                        wp[slot, at:at + 16, lo:lo + 128] = jnp.concatenate(
                            [blocks[2 * half][part], blocks[2 * half + 1][part]], axis=0).astype(BF)

    def finish(s, slot):
        prod = lax.dot_general(wp[slot, 0:64, :], wp[slot, 64:128, :], (((1,), (1,)), ((), ())), preferred_element_type=F32)
        sky[s, 0:32, :] = prod[0:32, 0:32] - prod[32:64, 32:64]
        sky[s, 32:64, :] = prod[0:32, 32:64] + prod[32:64, 0:32]

    def pair(i, _):
        one_subgrid(2 * i, 0)
        one_subgrid(2 * i + 1, 1)
        finish(2 * i, 0)
        finish(2 * i + 1, 1)
        return 0

    lax.fori_loop(first, last, pair, 0)


def pixel_ids():
    x = lax.broadcasted_iota(jnp.int32, (8, 128), 0)
    lane = lax.broadcasted_iota(jnp.int32, (8, 128), 1)
    return 4 * x + lax.shift_right_logical(lane, 5) - 16, (lane & 31) - 16


def fold_out(re, im, box, n):
    for y in range(4):
        ra = re if y == 0 else pltpu.roll(re, 128 - 32 * y, 1)
        rb = im if y == 0 else pltpu.roll(im, 128 - 32 * y, 1)
        box[n, pl.ds(y, 8, stride=4), :] = ra
        box[n, pl.ds(32 + y, 8, stride=4), :] = rb


WIDE = 4


def apply_boxes(sky, box, first):
    got = []
    for n in range(WIDE):
        kr, ki = box[n, 0:32, 0:32], box[n, 32:64, 0:32]
        got.append(cmul(sky[first + n, 0:32, :], sky[first + n, 32:64, :], kr, ki))
    return got


def step_screen(corner_ref, depth_ref, sky, box):
    p, q = pixel_ids()
    pf, qf = p.astype(F32), q.astype(F32)
    ap, aq = pf * F32(0.1 / 32), qf * F32(0.1 / 32)
    rad = ap * ap + aq * aq
    tp = (2.0 * pf + 1.0) * F32(1.0 / 32)
    tq = (2.0 * qf + 1.0) * F32(1.0 / 32)
    taper = (1.0 - tp * tp) * (1.0 - tq * tq) * F32(1.0 / math.sqrt(NK))

    def some(i, _):
        for n in range(WIDE):
            s = i * WIDE + n
            turn = (corner_ref[0, s] * p + corner_ref[1, s] * q) & 31
            ang = turn.astype(F32) * F32(2.0 * math.pi / 32) - F32(math.pi) * depth_ref[s] * rad
            fold_out(jnp.cos(ang) * taper, jnp.sin(ang) * taper, box, n)
        for n, pair in enumerate(apply_boxes(sky, box, i * WIDE)):
            sky[i * WIDE + n, 0:32, :] = pair[0]
            sky[i * WIDE + n, 32:64, :] = pair[1]
        return 0

    lax.fori_loop(0, NS // WIDE, some, 0)


def step_notes(au, corner_ref, lines, place):
    lines[...] = jnp.zeros_like(lines)
    lines[0:2, 0:NS] = corner_ref[...]
    row, col = lines[0:1, :], lines[1:2, :]
    dest = lax.shift_right_logical(col, 8)
    across = jnp.broadcast_to(dest.astype(F32), (128, 128))
    down = jnp.transpose(across)
    other = lax.broadcasted_iota(jnp.int32, (128, 128), 0)
    this = lax.broadcasted_iota(jnp.int32, (128, 128), 1)
    earlier = (down == across) & (other < this) & (other < NS)
    rank = jnp.sum(jnp.where(earlier, 1.0, 0.0), axis=0, keepdims=True)
    slot = jnp.where(this[0:1] < NS, dest.astype(F32) + 32.0 * rank, -1.0)
    chosen = (lax.broadcasted_iota(jnp.int32, (64, 128), 0).astype(F32) == slot).astype(BF)
    s = lax.broadcasted_iota(jnp.int32, (128, 32), 0)
    at = lax.broadcasted_iota(jnp.int32, (128, 32), 1)
    y, half = at & 15, lax.shift_right_logical(at, 4)
    for r in range(2):
        pick = (y < 12) & (s == y + 12 * (half if r == 0 else 1 - half))
        place[r * 32:r * 32 + 32, :] = jnp.dot(chosen[r * 32:r * 32 + 32], pick.astype(BF), preferred_element_type=F32).astype(BF)
    lines[0:1, :] = lax.shift_right_arithmetic(row - au * 512, 5)
    lines[1:2, :] = row & 31
    lines[2:3, :] = lax.shift_right_logical(col, 5)
    lines[3:4, :] = col & 31


def step_uv(station_ref, sky, table, lines, left_ref, right_ref, box, g_ref, rb):
    def spot(d):
        return ((d & 1) * 16 + lax.shift_right_logical(d, 5)) * 16 + (lax.shift_right_logical(d, 1) & 15)

    def some(i, _):
        for n in range(WIDE):
            s = i * WIDE + n
            a = table[spot(station_ref[0, s])].astype(F32)
            b = table[spot(station_ref[1, s])].astype(F32)
            pr = a[0:8] * b[0:8] + a[8:16] * b[8:16]
            pi_ = a[8:16] * b[0:8] - a[0:8] * b[8:16]
            fold_out(pr, pi_, box, n)
        for n, pair in enumerate(apply_boxes(sky, box, i * WIDE)):
            cor = jnp.concatenate(pair, axis=0).astype(BF)
            g = jnp.dot(left_ref[...], cor, preferred_element_type=F32)
            g_ref[pl.ds(pl.multiple_of((i * WIDE + n) * 64, 64), 64), :] = g.astype(BF)
        return 0

    lax.fori_loop(0, NS // WIDE, some, 0)

    for y in range(12):
        outs = []
        for half in range(2):
            s = y + 12 * half
            yv = jnp.dot(g_ref[s * 64:s * 64 + 64, :], right_ref[...], preferred_element_type=F32)
            outs.append(yv[0:32, 0:32] + yv[32:64, 32:64])
            outs.append(yv[32:64, 0:32] - yv[0:32, 32:64])
        rb[pl.ds(y, 32, stride=16), :] = jnp.concatenate(outs, axis=1)
    for n in range(4):
        rb[pl.ds(12 + n, 32, stride=16), :] = jnp.broadcast_to(lines[n:n + 1, :], (32, 128)).astype(F32)


def step_slots(rb, place, scr, slot_send):
    low = lax.broadcasted_iota(jnp.int32, (32, 128), 1) < 64

    def some(i, _):
        for n in range(4):
            c = i * 4 + n
            x = rb[pl.ds(pl.multiple_of(c * 16, 16), 16), :]
            both = jnp.concatenate([x, pltpu.roll(x, 64, 1)], axis=0).astype(BF)
            z = jnp.dot(place[...], both, preferred_element_type=F32)
            scr[pl.ds(c, 32, stride=32), :] = jnp.where(low, z[0:32], z[32:64])
        return 0

    lax.fori_loop(0, 8, some, 0)
    slot_send[...] = scr[...].reshape(32, 32, 128).astype(BF)


def step_rows(me, rows_recv, stage1_ref, twist_ref, scr, lhs, oht, yv, turned):
    scr[...] = rows_recv[...].reshape(512, 128).astype(F32)
    lane = lax.broadcasted_iota(jnp.int32, (32, 768), 1)
    src = lax.broadcasted_iota(jnp.int32, (32, 768), 0)
    pick_src = ((lane & 31) == src).astype(BF)
    pick_item = lax.shift_right_logical(lane, 5) == src

    def meta(n):
        table = jnp.transpose(scr[pl.ds(12 + n, 32, stride=16), :])[0:32]
        spread = jnp.dot(table.astype(BF), pick_src, preferred_element_type=F32)
        return jnp.sum(jnp.where(pick_item, spread, 0.0), axis=0, keepdims=True)

    g_hi, g_lo, h, e = [meta(n) for n in range(4)]
    g = g_hi + jnp.where(g_lo > me.astype(F32), 1.0, 0.0)
    h_id = lax.broadcasted_iota(jnp.int32, (256, 768), 0).astype(F32)
    oht[:, 0:768] = (h_id == h).astype(BF)
    oht[:, 768:1536] = (h_id == h + 1.0).astype(BF)
    col = (lax.broadcasted_iota(jnp.int32, (64, 384), 0) & 31).astype(F32)
    for half in range(2):
        parts = []
        for blk in range(3):
            rows = jnp.concatenate([scr[pl.ds(4 * blk + n, 32, stride=16), :] for n in range(4)], axis=0)
            parts.append(jnp.transpose(rows)[half * 64:half * 64 + 64])
        v = jnp.concatenate(parts, axis=1)
        at = half * 384
        first = col >= e[:, at:at + 384]
        hi = jnp.where(first, v, 0.0)
        lo = jnp.where(first, 0.0, v)
        for n in range(NG):
            here = g[:, at:at + 384] == float(n)
            lhs[n * 64:n * 64 + 64, at:at + 384] = jnp.where(here, hi, 0.0).astype(BF)
            lhs[n * 64:n * 64 + 64, 768 + at:768 + at + 384] = jnp.where(here, lo, 0.0).astype(BF)
    x = lax.dot_general(lhs[...], oht[...], (((1,), (1,)), ((), ())), preferred_element_type=F32).astype(BF)
    yv[...] = jnp.dot(x, stage1_ref[...], preferred_element_type=F32)
    for n in range(NG):
        y = yv[n * 64:n * 64 + 64, :]
        re = y[0:32, 0:256] - y[32:64, 256:512]
        im = y[0:32, 256:512] + y[32:64, 0:256]
        re, im = cmul(re, im, twist_ref[0], twist_ref[1])
        turned[n * 64:n * 64 + 64, :] = jnp.concatenate([re, im], axis=0).astype(BF)


def step_split(low, stage2_ref, turned, buf, sbuf, high_send, spill_send):
    for n in range(NG):
        if n == 16 and low == 1:
            continue
        at0, size = (low * 32, 32) if n < 16 else (0, 64)
        z = jnp.dot(stage2_ref[at0:at0 + size, :], turned[n * 64:n * 64 + 64, :], preferred_element_type=F32)
        for at in range(0, size, 16):
            comp = (at // 16) % 2
            for k in range(2):
                piece = z[at:at + 16, k * 128:k * 128 + 128]
                if n < 16:
                    buf[low * 2 + k, pl.ds(comp * 16 + n, 16, stride=32), :] = piece
                else:
                    sbuf[pl.ds(comp * 4 + (at // 32) * 2 + k, 16, stride=16), :] = piece
    for k in range(2):
        high_send[low, :, :, k * 128:k * 128 + 128] = buf[low * 2 + k].reshape(16, 32, 128).astype(BF)
    if low == 0:
        spill_send[...] = sbuf[...].reshape(16, 16, 128).astype(BF)


def step_high(me, low, high_recv, spill_recv, table_ref, xh, low_send):
    first = lax.broadcasted_iota(jnp.int32, (16, 256), 0) == 0
    for r in range(16):
        spill = spill_recv[(r + 15) % 16].astype(F32)
        for comp in range(2):
            block = high_recv[low, r, comp * 16:comp * 16 + 16, :].astype(F32)
            at = comp * 4 + low * 2
            line = jnp.concatenate([spill[at:at + 1], spill[at + 1:at + 2]], axis=1)
            xh[low, comp * 256 + r * 16:comp * 256 + r * 16 + 16, :] = jnp.where(first, block + line, block).astype(BF)
    y = lax.dot_general(xh[low], table_ref[...], (((0,), (0,)), ((), ())), preferred_element_type=F32)
    ql = lax.broadcasted_iota(jnp.int32, (8, 256), 1)
    ang = (ql * me).astype(F32) * F32(2.0 * math.pi / 8192)
    re, im = cmul(y[:, 0:256], y[:, 256:512], jnp.cos(ang)[0:1], jnp.sin(ang)[0:1])
    low_send[low * 16:low * 16 + 16, :, 0:256] = re.reshape(16, 16, 256).astype(BF)
    low_send[low * 16:low * 16 + 16, :, 256:512] = im.reshape(16, 16, 256).astype(BF)


def last_kernel(low_ref, tile_ref, table_ref, dirty_ref, grid_ref, held, scr, sems):
    take = pltpu.make_async_copy(tile_ref, held, sems.at[0])
    take.start()
    for k in range(4):
        scr[k] = low_ref[:, :, k * 128:k * 128 + 128].reshape(512, 128).astype(F32)

    def some(first):
        for m in range(first, first + 8):
            parts = [jnp.concatenate([scr[2 * comp + k, pl.ds(m, 32, stride=16), :] for k in range(2)], axis=1) for comp in range(2)]
            x = jnp.concatenate(parts, axis=0).astype(BF)
            z = jnp.dot(table_ref[...], x, preferred_element_type=F32) * F32(1.0 / (SUB * math.sqrt(12288)))
            for comp in range(2):
                for k in range(2):
                    dirty_ref[m, pl.ds(k * 2 + comp, 32, stride=4), :] = z[comp * 32:comp * 32 + 32, k * 128:k * 128 + 128]

    take.wait()
    give = pltpu.make_async_copy(held, grid_ref, sems.at[1])
    give.start()
    some(0)
    some(8)
    give.wait()


def last_call(low, tile):
    return pl.pallas_call(
        last_kernel,
        out_shape=(jax.ShapeDtypeStruct((16, 128, 128), F32), jax.ShapeDtypeStruct((2048, 128), F32)),
        in_specs=[VM, pl.BlockSpec(memory_space=pl.ANY), VM], out_specs=(VM, pl.BlockSpec(memory_space=pl.ANY)),
        scratch_shapes=[pltpu.VMEM((2048, 128), F32), pltpu.VMEM((4, 512, 128), F32), pltpu.SemaphoreType.DMA((2,))],
        name="last",
    )(low, tile, jnp.asarray(low_table(), BF))


def step_tile(me, scr, slot_recv, vals, spare, tile_ref, tail_send):
    vals[...] = slot_recv[...].reshape(1024, 128).astype(F32)
    hi, lo, h, e = [scr[pl.ds(12 + n, 32, stride=16), :] for n in range(4)]
    lane = lax.broadcasted_iota(jnp.int32, (32, 128), 1)
    base = me.astype(F32) * 8.0
    mine = (h >= base) & (h < base + 8.0) & (lane < NS)
    upto = (lax.broadcasted_iota(jnp.int32, (128, 128), 0) < lax.broadcasted_iota(jnp.int32, (128, 128), 1)).astype(BF)
    order = jnp.dot(mine.astype(BF), upto, preferred_element_type=F32)
    start = (h - base) * 32.0 + e
    column = lax.broadcasted_iota(jnp.int32, (32, 256), 1).astype(F32)
    seen, his, los = [], [], []
    for rank in range(2):
        pick = mine & (order == float(rank))
        hit = jnp.sum(jnp.where(pick, 1.0, 0.0), axis=1, keepdims=True)
        low_edge = jnp.sum(jnp.where(pick, start, 0.0), axis=1, keepdims=True)
        seen.append((column >= low_edge) & (column < low_edge + 32.0 * hit))
        for box, values in ((his, hi), (los, lo)):
            one = jnp.sum(jnp.where(pick, values, 0.0), axis=1, keepdims=True)
            box.append(jnp.transpose(jnp.broadcast_to(one, (32, 128)))[0:1, :])
    hi_line = jnp.concatenate(his, axis=1)
    lo_line = jnp.concatenate(los, axis=1)
    g_id = lax.broadcasted_iota(jnp.int32, (32, 64), 0).astype(F32)
    quarter = lax.shift_right_logical(lane, 5)

    def place_row(c):
        x = vals[pl.ds(c, 32, stride=32), :]
        lines = []
        for rank in range(2):
            for comp in range(2):
                y = jnp.where(quarter == rank * 2 + comp, x, 0.0)
                y = y + pltpu.roll(y, 32, 1)
                y = y + pltpu.roll(y, 64, 1)
                lines.append(jnp.where(seen[rank], jnp.concatenate([y, y], axis=1), 0.0))
        rhs = jnp.concatenate([jnp.concatenate(lines[0:2], axis=1), jnp.concatenate(lines[2:4], axis=1)], axis=0).astype(BF)
        where = hi_line + jnp.where(lo_line > c.astype(F32), 1.0, 0.0)
        z = jnp.dot((g_id == where).astype(BF), rhs, preferred_element_type=F32)
        for comp in range(2):
            for half in range(2):
                at = comp * 2 + half
                tile_ref[pl.ds(c * 4 + half * 2 + comp, 16, stride=128), :] = z[0:16, at * 128:at * 128 + 128]
                spare[at, pl.ds(pl.multiple_of(c * 8, 8), 8), :] = z[16:24, at * 128:at * 128 + 128]

    def some(i, _):
        place_row(i * 2)
        place_row(i * 2 + 1)
        return 0

    lax.fori_loop(0, 16, some, 0)
    for k in range(4):
        tail_send[k] = spare[k, pl.ds(0, 32, stride=8), :].astype(BF)


MESH = pl.DeviceIdType.MESH
SPLIT = 8


def whole_kernel(corner_ref, station_ref, depth_ref, scale_ref, corner_vec, vis_ref, off_ref, beam_ref,
                 left_ref, right_ref, stage1_ref, twist_ref, stage2_ref, high_ref,
                 low_out, tile_out,
                 table, zu, mu, zv, wp, sky, box, g_ref, rb, rows_send, rows_recv, scr, lhs, oht, yv, buf, sbuf,
                 high_send, high_recv, spill_send, spill_recv, xh, low_send, low_recv, slot_scr, slot_send, slot_recv,
                 spare, tail_send, tail_recv, vs, lines, place, own_beam, turned, tile_ref, sem1, sem2, sem3, sem4, sem5, sem6, sem7, sem8, sem9, local_sem):
    au, me = lax.axis_index("au"), lax.axis_index("vert")
    z, core = me // 2, me % 2
    NZ, NA, NV = 16, 16, 32

    def remote(src, dst, sems, k, to):
        return pltpu.make_async_remote_copy(src_ref=src, dst_ref=dst, send_sem=sems.at[0, k], recv_sem=sems.at[1, k],
                                            device_id=to, device_id_type=MESH)

    def loop(first, last, body):
        lax.fori_loop(first, last, lambda k, _: (body(k), 0)[1], 0)

    barrier = pltpu.get_barrier_semaphore()
    loop(1, NV, lambda k: pl.semaphore_signal(barrier, inc=1, device_id=(au, (me + k) % NV), device_id_type=MESH))
    loop(1, NA, lambda k: pl.semaphore_signal(barrier, inc=1, device_id=((au + k) % NA, me), device_id_type=MESH))

    def spot(core, au, z):
        return (core * NA + au) * NZ + z

    def along_z(k, back):
        peer = (z + NZ - k) % NZ if back else (z + k) % NZ
        return remote(own_beam, table.at[spot(core, au, peer if back else z)], sem1, k, (au, peer * 2 + core))

    def over_au(k, back):
        peer = (au + NA - k) % NA if back else (au + k) % NA
        at = table.at[pl.ds(spot(core, peer if back else au, 0), NZ)]
        return remote(at, at, sem2, k, (peer, me))

    def partner(k, back):
        at = table.at[pl.ds(spot(1 - core if back else core, (au + NA - k) % NA, 0), NZ)]
        return remote(at, at, sem3, k, (au, z * 2 + 1 - core))

    box[0, 0:16, :] = beam_ref[...].astype(F32)
    own_beam[...] = jnp.concatenate([box[0, pl.ds(0, 8, stride=2), :], box[0, pl.ds(1, 8, stride=2), :]], axis=0).astype(BF)
    own = pltpu.make_async_copy(own_beam, table.at[spot(core, au, z)], local_sem.at[0])
    own.start()
    pl.semaphore_wait(barrier, NV - 1 + NA - 1)
    loop(1, NZ, lambda k: along_z(k, False).start())
    step_setup(vis_ref, off_ref, scale_ref, vs, zu, mu, zv)
    step_sky(0, SPLIT, zu, mu, zv, wp, sky)
    own.wait()
    loop(1, NZ, lambda k: along_z(k, True).wait_recv())
    loop(1, NA, lambda k: over_au(k, False).start())
    partner(0, False).start()
    step_sky(SPLIT, 12, zu, mu, zv, wp, sky)
    step_notes(au, corner_vec, lines, place)
    step_screen(corner_ref, depth_ref, sky, box)

    def relay(k):
        over_au(k, True).wait_recv()
        partner(k, False).start()

    loop(1, NA, relay)
    loop(0, NA, lambda k: partner(k, True).wait_recv())
    step_uv(station_ref, sky, table, lines, left_ref, right_ref, box, g_ref, rb)
    rows_send[...] = rb[...].reshape(32, 16, 128).astype(BF)

    def along_vert(send, recv, sems, k, back):
        peer = (me + NV - k) % NV if back else (me + k) % NV
        return remote(send.at[peer], recv.at[peer if back else me], sems, k, (au, peer))

    def across_au(send, recv, sems, k, back):
        peer = (au + NA - k) % NA if back else (au + k) % NA
        return remote(send.at[peer], recv.at[peer if back else au], sems, k, (peer, me))

    loop(1, NV, lambda k: along_vert(rows_send, rows_recv, sem4, k, False).start())
    rows_recv[me] = rows_send[me]
    step_slots(rb, place, slot_scr, slot_send)
    loop(1, NV, lambda k: along_vert(slot_send, slot_recv, sem5, k, False).start())
    slot_recv[me] = slot_send[me]
    loop(1, NV, lambda k: along_vert(rows_send, rows_recv, sem4, k, True).wait_recv())
    step_rows(me, rows_recv, stage1_ref, twist_ref, scr, lhs, oht, yv, turned)

    def half_across(low, k, back):
        peer = (au + NA - k) % NA if back else (au + k) % NA
        return remote(high_send.at[low, peer], high_recv.at[low, peer if back else au], sem6, low * NA + k, (peer, me))

    for low in range(2):
        step_split(low, stage2_ref, turned, buf, sbuf, high_send, spill_send)
        loop(1, NA, lambda k: half_across(low, k, False).start())
        high_recv[low, au] = high_send[low, au]
        if low == 0:
            loop(1, NA, lambda k: across_au(spill_send, spill_recv, sem7, k, False).start())
            spill_recv[au] = spill_send[au]
    loop(1, NA, lambda k: across_au(spill_send, spill_recv, sem7, k, True).wait_recv())
    for low in range(2):
        loop(1, NA, lambda k: half_across(low, k, True).wait_recv())
        step_high(me, low, high_recv, spill_recv, high_ref, xh, low_send)

        def send_low(k):
            @pl.when(((me + k) % NV) // 16 == low)
            def _():
                along_vert(low_send, low_recv, sem8, k, False).start()

        loop(1, NV, send_low)
    low_recv[me] = low_send[me]
    loop(1, NV, lambda k: along_vert(slot_send, slot_recv, sem5, k, True).wait_recv())
    step_tile(me, scr, slot_recv, slot_scr, spare, tile_ref, tail_send)
    tail = remote(tail_send, tail_recv, sem9, 0, ((au + 1) % NA, me))
    tail.start()
    tail.wait_recv()
    for k in range(4):
        tile_ref[pl.ds((k % 2) * 2 + k // 2, 32, stride=4), :] += tail_recv[k].astype(F32)
    put_tile = pltpu.make_async_copy(tile_ref, tile_out, local_sem.at[1])
    put_tile.start()
    loop(1, NV, lambda k: along_vert(low_send, low_recv, sem8, k, True).wait_recv())
    put_low = pltpu.make_async_copy(low_recv, low_out, local_sem.at[2])
    put_low.start()

    loop(1, NZ, lambda k: along_z(k, False).wait_send())
    loop(1, NA, lambda k: over_au(k, False).wait_send())
    loop(0, NA, lambda k: partner(k, False).wait_send())
    loop(1, NV, lambda k: along_vert(rows_send, rows_recv, sem4, k, False).wait_send())
    loop(1, NV, lambda k: along_vert(slot_send, slot_recv, sem5, k, False).wait_send())
    for low in range(2):
        loop(1, NA, lambda k: half_across(low, k, False).wait_send())
    loop(1, NA, lambda k: across_au(spill_send, spill_recv, sem7, k, False).wait_send())
    loop(1, NV, lambda k: along_vert(low_send, low_recv, sem8, k, False).wait_send())
    tail.wait_send()
    put_tile.wait()
    put_low.wait()


def whole_call(corners, stations, depth, scale, vis, off, beam):
    left, right = dft_tables()
    stage1, twist, stage2 = row_tables()
    consts = [jnp.asarray(left, BF), jnp.asarray(right, BF), jnp.asarray(stage1, BF), jnp.asarray(twist, F32),
              jnp.asarray(stage2, BF), jnp.asarray(high_table(), BF)]
    V, D = pltpu.VMEM, pltpu.SemaphoreType.DMA
    scratch = [
        V((512, 16, 128), BF), V((6, 16, 32, 128), F32), V((8, 16, 32, 128), F32), V((10, 16, 32, 128), F32), V((2, 128, NK), BF),
        V((NS, 64, 32), F32), V((WIDE, 64, 128), F32), V((NS * 64, 32), BF), V((512, 128), F32), V((32, 16, 128), BF), V((32, 16, 128), BF),
        V((512, 128), F32), V((NG * 64, 1536), BF), V((256, 1536), BF), V((NG * 64, 512), F32), V((4, 512, 128), F32), V((256, 128), F32),
        V((2, 16, 32, 256), BF), V((2, 16, 32, 256), BF), V((16, 16, 128), BF), V((16, 16, 128), BF), V((2, 512, 256), BF),
        V((32, 16, 512), BF), V((32, 16, 512), BF), V((1024, 128), F32), V((32, 32, 128), BF), V((32, 32, 128), BF),
        V((4, 256, 128), F32), V((4, 32, 128), BF), V((4, 32, 128), BF),
        V((768, 128), F32), V((8, 128), jnp.int32), V((64, 32), BF), V((16, 128), BF), V((NG * 64, 256), BF), V((2048, 128), F32),
        D((2, 16)), D((2, 16)), D((2, 16)), D((2, 32)), D((2, 32)), D((2, 32)), D((2, 16)), D((2, 32)), D((2, 1)), D((3,)),
    ]
    return pl.pallas_call(
        whole_kernel,
        out_shape=(jax.ShapeDtypeStruct((32, 16, 512), BF), jax.ShapeDtypeStruct((2048, 128), F32)),
        in_specs=[SM] * 4 + [VM] * 10, out_specs=(pl.BlockSpec(memory_space=pl.ANY),) * 2,
        scratch_shapes=scratch,
        compiler_params=pltpu.CompilerParams(collective_id=0, has_side_effects=True, vmem_limit_bytes=60 << 20),
        name="whole",
    )(corners, stations, depth, scale, corners, vis, off, beam, *consts)


def on_device(visibilities, baseline_offsets, channel_scale, screen_depth, stations, corners, beam_terms):
    low, tile = whole_call(
        corners.T, stations.T, screen_depth, channel_scale,
        visibilities.reshape(NS, 2, 16, 128).transpose(0, 2, 1, 3).reshape(768, 128),
        baseline_offsets.reshape(48, 128),
        beam_terms.reshape(2, 8, 128).transpose(1, 0, 2).reshape(16, 128),
    )
    dirty, tile = last_call(low, tile)
    gridded = tile.reshape(512, 2, 2, 128).transpose(0, 2, 1, 3).reshape(512, 2, 256)
    return gridded, dirty.reshape(16, 64, 2, 128).transpose(0, 2, 1, 3).reshape(16, 2, 8192)


def solution(mesh):
    from jax.sharding import PartitionSpec as P

    both = ("au", "vert")
    return jax.shard_map(
        on_device,
        mesh=mesh,
        in_specs=(P(both, None, None), P(both, None, None), P(), P(both), P(both, None), P(both, None), P(both, None, None)),
        out_specs=(P("au", None, "vert"), P(both, None, None)),
        check_vma=False,
    )
```

time: 129 us -> 101 us (0.78)
  the two profiles are of different devices: /device:TPU:1 before, /device:TPU:8 now
where the time goes in v3:
time: 101 us; the launch traced here: 100 us
  Pallas kernels  99.7 us (99%)
    pallas_call x1, Pallas kernels, whole_call(): pl.pallas_call(whole_kernel, out_shape=(jax.ShapeDtypeStruct((32, 16, 512...  95.5 us
    pallas_call x1, Pallas kernels, last_call(): pl.pallas_call(last_kernel, out_shape=(jax.ShapeDtypeStruct((16, 128, 128...  4.23 us

profile of v3, /device:TPU:8, one launch (start us, length us, event | category | flops | bytes accessed | tf_op | source)
XLA Modules:
  0.0 100.4 jit_solution(4800595421183642450)
XLA Ops:
  0.6 95.5 %whole.1 = (bf16[32,16,512]{2,1,0:T(8,128)(2,1)}, f32[2048,128]{1,0:T(8,128)}) custom-call(s32[2,24]{1,0:T(2,128)} %bitcast.26, s32[2,24]{1,0:T(2,128)} %bitcast.28, f32[24]{0:T(128)} %depth_ref.1, f32[16]{0:T(128)} %scale_ref.1, s32[2,24]{1,0:T(2,128)} %bitcast.27, bf16[768,128]{1,0:T(8,128)(2,1)} %bitcast.23, f32[48,128]{1,0:T(8,128)} %bitcast.24, ...), custom_call_target="tpu_custom_call" | custom-call | tf_op jit(solution)/shard_map/whole/pallas_call | solution.py:590
  96.1 4.2 %last.1 = (f32[16,128,128]{2,1,0:T(8,128)}, f32[2048,128]{1,0:T(8,128)}) custom-call(bf16[32,16,512]{2,1,0:T(8,128)(2,1)} %get-tuple-element.6.low_ref, f32[2048,128]{1,0:T(8,128)} %get-tuple-element.7.tile_ref, bf16[64,64]{1,0:T(8,128)(2,1)} %constant.20.clone.table_ref), custom_call_target="tpu_custom_call" | custom-call | tf_op jit(solution)/shard_map/last/pallas_call | solution.py:381

commit v4 on v3

--- a/solution.py
+++ b/solution.py
@@ -228,14 +228,14 @@
 
 
 def step_uv(station_ref, sky, table, lines, left_ref, right_ref, box, g_ref, rb):
-    def spot(d):
-        return ((d & 1) * 16 + lax.shift_right_logical(d, 5)) * 16 + (lax.shift_right_logical(d, 1) & 15)
+    def beam(d):
+        return table[d & 1, lax.shift_right_logical(d, 7), lax.shift_right_logical(d, 5) & 3, lax.shift_right_logical(d, 1) & 15].astype(F32)
 
     def some(i, _):
         for n in range(WIDE):
             s = i * WIDE + n
-            a = table[spot(station_ref[0, s])].astype(F32)
-            b = table[spot(station_ref[1, s])].astype(F32)
+            a = beam(station_ref[0, s])
+            b = beam(station_ref[1, s])
             pr = a[0:8] * b[0:8] + a[8:16] * b[8:16]
             pi_ = a[8:16] * b[0:8] - a[0:8] * b[8:16]
             fold_out(pr, pi_, box, n)
@@ -464,25 +464,38 @@
     loop(1, NV, lambda k: pl.semaphore_signal(barrier, inc=1, device_id=(au, (me + k) % NV), device_id_type=MESH))
     loop(1, NA, lambda k: pl.semaphore_signal(barrier, inc=1, device_id=((au + k) % NA, me), device_id_type=MESH))
 
-    def spot(core, au, z):
-        return (core * NA + au) * NZ + z
+    y, x = au // 4, au % 4
+
+    def less(a, k):
+        return (a + 4 - k) % 4
 
     def along_z(k, back):
         peer = (z + NZ - k) % NZ if back else (z + k) % NZ
-        return remote(own_beam, table.at[spot(core, au, peer if back else z)], sem1, k, (au, peer * 2 + core))
-
-    def over_au(k, back):
-        peer = (au + NA - k) % NA if back else (au + k) % NA
-        at = table.at[pl.ds(spot(core, peer if back else au, 0), NZ)]
-        return remote(at, at, sem2, k, (peer, me))
-
-    def partner(k, back):
-        at = table.at[pl.ds(spot(1 - core if back else core, (au + NA - k) % NA, 0), NZ)]
-        return remote(at, at, sem3, k, (au, z * 2 + 1 - core))
+        return remote(own_beam, table.at[core, y, x, peer if back else z], sem1, k, (au, peer * 2 + core))
+
+    def over_x(k, back):
+        at = table.at[core, y, less(x, k) if back else x]
+        return remote(at, at, sem2, k, (y * 4 + (x + k) % 4, me))
+
+    def over_y(k, back):
+        at = table.at[core, less(y, k) if back else y, x]
+        return remote(at, at, sem2, 4 + k, ((y + k) % 4 * 4 + x, me))
+
+    def relay_y(k, j, back):
+        at = table.at[core, less(y, j) if back else y, less(x, k), pl.ds(0, 8)]
+        return remote(at, at, sem2, 8 + (k - 1) * 3 + j - 1, ((y + j) % 4 * 4 + x, me))
+
+    def relay_x(k, j, back):
+        at = table.at[core, less(y, k), less(x, j) if back else x, pl.ds(8, 8)]
+        return remote(at, at, sem2, 17 + (k - 1) * 3 + j - 1, (y * 4 + (x + j) % 4, me))
+
+    def partner(dy, dx, back):
+        at = table.at[1 - core if back else core, less(y, dy), less(x, dx)]
+        return remote(at, at, sem3, dy * 4 + dx, (au, z * 2 + 1 - core))
 
     box[0, 0:16, :] = beam_ref[...].astype(F32)
     own_beam[...] = jnp.concatenate([box[0, pl.ds(0, 8, stride=2), :], box[0, pl.ds(1, 8, stride=2), :]], axis=0).astype(BF)
-    own = pltpu.make_async_copy(own_beam, table.at[spot(core, au, z)], local_sem.at[0])
+    own = pltpu.make_async_copy(own_beam, table.at[core, y, x, z], local_sem.at[0])
     own.start()
     pl.semaphore_wait(barrier, NV - 1 + NA - 1)
     loop(1, NZ, lambda k: along_z(k, False).start())
@@ -490,18 +503,30 @@
     step_sky(0, SPLIT, zu, mu, zv, wp, sky)
     own.wait()
     loop(1, NZ, lambda k: along_z(k, True).wait_recv())
-    loop(1, NA, lambda k: over_au(k, False).start())
-    partner(0, False).start()
+    for k in (1, 2, 3):
+        over_x(k, False).start()
+        over_y(k, False).start()
+    partner(0, 0, False).start()
     step_sky(SPLIT, 12, zu, mu, zv, wp, sky)
+    for k in (1, 3, 2):
+        over_x(k, True).wait_recv()
+        for j in (1, 2, 3):
+            relay_y(k, j, False).start()
+        over_y(k, True).wait_recv()
+        for j in (1, 2, 3):
+            relay_x(k, j, False).start()
+        partner(0, k, False).start()
+        partner(k, 0, False).start()
     step_notes(au, corner_vec, lines, place)
     step_screen(corner_ref, depth_ref, sky, box)
-
-    def relay(k):
-        over_au(k, True).wait_recv()
-        partner(k, False).start()
-
-    loop(1, NA, relay)
-    loop(0, NA, lambda k: partner(k, True).wait_recv())
+    for dy in (1, 3, 2):
+        for dx in (1, 3, 2):
+            relay_y(dx, dy, True).wait_recv()
+            relay_x(dy, dx, True).wait_recv()
+            partner(dy, dx, False).start()
+    for dy in range(4):
+        for dx in range(4):
+            partner(dy, dx, True).wait_recv()
     step_uv(station_ref, sky, table, lines, left_ref, right_ref, box, g_ref, rb)
     rows_send[...] = rb[...].reshape(32, 16, 128).astype(BF)
 
@@ -558,8 +583,15 @@
     put_low.start()
 
     loop(1, NZ, lambda k: along_z(k, False).wait_send())
-    loop(1, NA, lambda k: over_au(k, False).wait_send())
-    loop(0, NA, lambda k: partner(k, False).wait_send())
+    for k in (1, 2, 3):
+        over_x(k, False).wait_send()
+        over_y(k, False).wait_send()
+        for j in (1, 2, 3):
+            relay_y(k, j, False).wait_send()
+            relay_x(k, j, False).wait_send()
+    for dy in range(4):
+        for dx in range(4):
+            partner(dy, dx, False).wait_send()
     loop(1, NV, lambda k: along_vert(rows_send, rows_recv, sem4, k, False).wait_send())
     loop(1, NV, lambda k: along_vert(slot_send, slot_recv, sem5, k, False).wait_send())
     for low in range(2):
@@ -578,14 +610,14 @@
               jnp.asarray(stage2, BF), jnp.asarray(high_table(), BF)]
     V, D = pltpu.VMEM, pltpu.SemaphoreType.DMA
     scratch = [
-        V((512, 16, 128), BF), V((6, 16, 32, 128), F32), V((8, 16, 32, 128), F32), V((10, 16, 32, 128), F32), V((2, 128, NK), BF),
+        V((2, 4, 4, 16, 16, 128), BF), V((6, 16, 32, 128), F32), V((8, 16, 32, 128), F32), V((10, 16, 32, 128), F32), V((2, 128, NK), BF),
         V((NS, 64, 32), F32), V((WIDE, 64, 128), F32), V((NS * 64, 32), BF), V((512, 128), F32), V((32, 16, 128), BF), V((32, 16, 128), BF),
         V((512, 128), F32), V((NG * 64, 1536), BF), V((256, 1536), BF), V((NG * 64, 512), F32), V((4, 512, 128), F32), V((256, 128), F32),
         V((2, 16, 32, 256), BF), V((2, 16, 32, 256), BF), V((16, 16, 128), BF), V((16, 16, 128), BF), V((2, 512, 256), BF),
         V((32, 16, 512), BF), V((32, 16, 512), BF), V((1024, 128), F32), V((32, 32, 128), BF), V((32, 32, 128), BF),
         V((4, 256, 128), F32), V((4, 32, 128), BF), V((4, 32, 128), BF),
         V((768, 128), F32), V((8, 128), jnp.int32), V((64, 32), BF), V((16, 128), BF), V((NG * 64, 256), BF), V((2048, 128), F32),
-        D((2, 16)), D((2, 16)), D((2, 16)), D((2, 32)), D((2, 32)), D((2, 32)), D((2, 16)), D((2, 32)), D((2, 1)), D((3,)),
+        D((2, 16)), D((2, 32)), D((2, 16)), D((2, 32)), D((2, 32)), D((2, 32)), D((2, 16)), D((2, 32)), D((2, 1)), D((3,)),
     ]
     return pl.pallas_call(
         whole_kernel,

time: 101 us -> 96.5 us (0.955)
  the two profiles are of different devices: /device:TPU:8 before, /device:TPU:1 now
where the time goes in v4:
time: 96.5 us; the launch traced here: 96.3 us
  Pallas kernels  95.6 us (99%)
    pallas_call x1, Pallas kernels, whole_call(): pl.pallas_call(whole_kernel, out_shape=(jax.ShapeDtypeStruct((32, 16, 512...  91.4 us
    pallas_call x1, Pallas kernels, last_call(): pl.pallas_call(last_kernel, out_shape=(jax.ShapeDtypeStruct((16, 128, 128...  4.23 us

profile of v4, /device:TPU:1, one launch (start us, length us, event | category | flops | bytes accessed | tf_op | source)
XLA Modules:
  0.0 96.3 jit_solution(3862699525756675141)
XLA Ops:
  0.6 91.4 %whole.1 = (bf16[32,16,512]{2,1,0:T(8,128)(2,1)}, f32[2048,128]{1,0:T(8,128)}) custom-call(s32[2,24]{1,0:T(2,128)} %bitcast.26, s32[2,24]{1,0:T(2,128)} %bitcast.28, f32[24]{0:T(128)} %depth_ref.1, f32[16]{0:T(128)} %scale_ref.1, s32[2,24]{1,0:T(2,128)} %bitcast.27, bf16[768,128]{1,0:T(8,128)(2,1)} %bitcast.23, f32[48,128]{1,0:T(8,128)} %bitcast.24, ...), custom_call_target="tpu_custom_call" | custom-call | tf_op jit(solution)/shard_map/whole/pallas_call | solution.py:622
  92.0 4.2 %last.1 = (f32[16,128,128]{2,1,0:T(8,128)}, f32[2048,128]{1,0:T(8,128)}) custom-call(bf16[32,16,512]{2,1,0:T(8,128)(2,1)} %get-tuple-element.6.low_ref, f32[2048,128]{1,0:T(8,128)} %get-tuple-element.7.tile_ref, bf16[64,64]{1,0:T(8,128)(2,1)} %constant.20.clone.table_ref), custom_call_target="tpu_custom_call" | custom-call | tf_op jit(solution)/shard_map/last/pallas_call | solution.py:381
